TPU v7x, 32 devices: a whole 2x2x4 slice. The times are simulated.
32 devices in a mesh: rep: 16 (over z, y, x), shard: 2 (over core).
Axes of the slice: x: 2, y: 2, z: 4, core: 2. Of those that a mesh axis runs over, the one named last changes fastest.
Arguments:
- layer_input: bfloat16 [4096, 1024], P(('rep', 'shard')), may hold values from -6 to 6
- cotangent: bfloat16 [4096, 1024], P(('rep', 'shard')), may hold values from -6 to 6
- w_qkv: float32 [1024, 3072], P('shard'), may hold values from -0.1875 to 0.1875
- qv_bias: float32 [2, 1024], P(None, 'shard'), may hold values from -2 to 2
- w_out: float32 [1024, 1024], P('shard'), may hold values from -0.1875 to 0.1875
- out_bias: float32 [1024], P('shard'), may hold values from -2 to 2
- head_scale: float32 [16], P('shard'), may hold values from 0.5 to 2
- ln1_gain: float32 [1024], P('shard'), may hold values from 0.5 to 1.5
- ln1_bias: float32 [1024], P('shard'), may hold values from -2 to 2
- ln2_gain: float32 [1024], P('shard'), may hold values from 0.5 to 1.5
- ln2_bias: float32 [1024], P('shard'), may hold values from -2 to 2
- ln3_gain: float32 [1024], P('shard'), may hold values from 0.5 to 1.5
- ln3_bias: float32 [1024], P('shard'), may hold values from -2 to 2
- w_fc1: float32 [1024, 4096], P('shard'), may hold values from -0.1875 to 0.1875
- fc1_bias: float32 [4096], P('shard'), may hold values from -2 to 2
- ln4_gain: float32 [4096], P('shard'), may hold values from 0.5 to 1.5
- ln4_bias: float32 [4096], P('shard'), may hold values from -2 to 2
- w_fc2: float32 [4096, 1024], P('shard'), may hold values from -0.09375 to 0.09375
- fc2_bias: float32 [1024], P('shard'), may hold values from -2 to 2
Outputs:
- output: bfloat16 [4096, 1024], P(('rep', 'shard'))
- grad_input: float32 [4096, 1024], P(('rep', 'shard'))
- grad_w_qkv: float32 [1024, 3072], P('shard')
- grad_qv_bias: float32 [2, 1024], P(None, 'shard')
- grad_w_out: float32 [1024, 1024], P('shard')
- grad_out_bias: float32 [1024], P('shard')
- grad_head_scale: float32 [16], P('shard')
- grad_ln1_gain: float32 [1024], P('shard')
- grad_ln1_bias: float32 [1024], P('shard')
- grad_ln2_gain: float32 [1024], P('shard')
- grad_ln2_bias: float32 [1024], P('shard')
- grad_ln3_gain: float32 [1024], P('shard')
- grad_ln3_bias: float32 [1024], P('shard')
- grad_w_fc1: float32 [1024, 4096], P('shard')
- grad_fc1_bias: float32 [4096], P('shard')
- grad_ln4_gain: float32 [4096], P('shard')
- grad_ln4_bias: float32 [4096], P('shard')
- grad_w_fc2: float32 [4096, 1024], P('shard')
- grad_fc2_bias: float32 [1024], P('shard')
All inputs are finite; a program needn't handle non-finite values.
Results may differ from a plain program's by a relative error of at most 0.012.
The roundings to bfloat16 on the way count: a program that leaves them out, or rounds other values in their place, can miss the bound.
Values may be sent and summed in bfloat16 or wider, within the bound.
A program may use at most 320 MiB of HBM per device.

v0:
```python
import functools

import jax
import jax.numpy as jnp
from jax import lax
from jax.experimental import pallas as pl
from jax.experimental.pallas import tpu as pltpu
from jax.sharding import PartitionSpec as P

D = 1024
HEADS = 16
HEAD_DIM = 64


EPS = 1e-05
NEG = -1e30


def norm_rows(v, gain, bias):
    centre = jnp.mean(v, axis=-1, keepdims=True)
    centred = v - centre
    spread = jnp.mean(centred * centred, axis=-1, keepdims=True)
    return centred * lax.rsqrt(spread + EPS) * gain + bias


def ffn_middle(hidden, gain, bias):
    return norm_rows(jax.nn.gelu(hidden, approximate=False), gain, bias)


def causal_mask(index, qblock, length):
    rows = index * qblock + lax.iota(jnp.int32, qblock)
    cols = lax.iota(jnp.int32, length)
    return (cols[None, :] <= rows[:, None])[None]


def block_scores(queries, keys_all, index, qblock, scale):
    length = keys_all.shape[0]
    scores = (
        jnp.einsum("qhd,khd->hqk", queries, keys_all, preferred_element_type=jnp.float32) * scale
    )
    return (queries, jnp.where(causal_mask(index, qblock, length), scores, NEG))


def attend_forward(queries, keys_all, values_all, scale):
    length, heads, width = queries.shape
    qblock = min(512, length)
    blocks = length // qblock

    def one_block(index):
        rows_q, scores = block_scores(queries, keys_all, index, qblock, scale)
        total = jax.nn.logsumexp(scores, axis=-1, keepdims=True)
        probs = jnp.exp(scores - total).astype(jnp.bfloat16)
        outcome = jnp.einsum("hqk,khd->qhd", probs, values_all, preferred_element_type=jnp.float32)
        return (outcome, total)

    outcome, totals = lax.map(one_block, jnp.arange(blocks, dtype=jnp.int32))
    return (outcome.reshape(length, heads, width), totals)


def attend_backward(queries, keys_all, values_all, totals, grad_out, scale):
    length, heads, width = queries.shape
    qblock = min(512, length)
    blocks = length // qblock

    def one_block(carry, index):
        grad_keys, grad_values = carry
        rows_q, scores = block_scores(queries, keys_all, index, qblock, scale)
        probs = jnp.exp(scores - totals[index])
        probs_low = probs.astype(jnp.bfloat16)
        grad_values = grad_values + jnp.einsum(
            "hqk,qhd->khd", probs_low, grad_out, preferred_element_type=jnp.float32
        )
        grad_probs = jnp.einsum(
            "qhd,khd->hqk", grad_out, values_all, preferred_element_type=jnp.float32
        )
        row_dot = jnp.sum(probs * grad_probs, axis=-1, keepdims=True)
        grad_scores = (probs * (grad_probs - row_dot)).astype(jnp.bfloat16)
        grad_rows = (
            jnp.einsum("hqk,khd->qhd", grad_scores, keys_all, preferred_element_type=jnp.float32)
            * scale
        )
        grad_keys = (
            grad_keys
            + jnp.einsum("hqk,qhd->khd", grad_scores, rows_q, preferred_element_type=jnp.float32)
            * scale
        )
        return ((grad_keys, grad_values), grad_rows)

    empty = jnp.zeros((length, heads, width), jnp.float32)
    (grad_keys, grad_values), grad_queries = lax.scan(
        one_block, (empty, empty), jnp.arange(blocks, dtype=jnp.int32)
    )
    return (grad_queries.reshape(length, heads, width), grad_keys, grad_values)


def on_any_mesh(
    layer_input,
    cotangent,
    w_qkv,
    qv_bias,
    w_out,
    out_bias,
    head_scale,
    ln1_gain,
    ln1_bias,
    ln2_gain,
    ln2_bias,
    ln3_gain,
    ln3_bias,
    w_fc1,
    fc1_bias,
    ln4_gain,
    ln4_bias,
    w_fc2,
    fc2_bias,
):
    low_qkv = w_qkv.astype(jnp.bfloat16)
    low_out = w_out.astype(jnp.bfloat16)
    low_heads = head_scale.astype(jnp.bfloat16)
    low_up = w_fc1.astype(jnp.bfloat16)
    low_down = w_fc2.astype(jnp.bfloat16)
    whole = (
        lax.all_gather(low_qkv, "shard", axis=0, tiled=True),
        lax.all_gather(qv_bias.astype(jnp.bfloat16), "shard", axis=1, tiled=True),
        lax.all_gather(low_out, "shard", axis=0, tiled=True),
        lax.all_gather(out_bias.astype(jnp.bfloat16), "shard", axis=0, tiled=True),
        lax.all_gather(low_heads, "shard", axis=0, tiled=True),
        lax.all_gather(ln1_gain.astype(jnp.bfloat16), "shard", axis=0, tiled=True),
        lax.all_gather(ln1_bias.astype(jnp.bfloat16), "shard", axis=0, tiled=True),
        lax.all_gather(ln2_gain.astype(jnp.bfloat16), "shard", axis=0, tiled=True),
        lax.all_gather(ln2_bias.astype(jnp.bfloat16), "shard", axis=0, tiled=True),
        lax.all_gather(ln3_gain.astype(jnp.bfloat16), "shard", axis=0, tiled=True),
        lax.all_gather(ln3_bias.astype(jnp.bfloat16), "shard", axis=0, tiled=True),
        lax.all_gather(low_up, "shard", axis=0, tiled=True),
        lax.all_gather(fc1_bias.astype(jnp.bfloat16), "shard", axis=0, tiled=True),
        lax.all_gather(ln4_gain.astype(jnp.bfloat16), "shard", axis=0, tiled=True),
        lax.all_gather(ln4_bias.astype(jnp.bfloat16), "shard", axis=0, tiled=True),
        lax.all_gather(low_down, "shard", axis=0, tiled=True),
        lax.all_gather(fc2_bias.astype(jnp.bfloat16), "shard", axis=0, tiled=True),
    )
    weight_qkv, weight_out, weight_up, weight_down = (whole[0], whole[2], whole[11], whole[15])
    (
        bias_qv,
        bias_out,
        head_gain,
        gain_one,
        shift_one,
        gain_two,
        shift_two,
        gain_three,
        shift_three,
        bias_up,
        gain_four,
        shift_four,
        bias_down,
    ) = tuple(
        (whole[index].astype(jnp.float32) for index in (1, 3, 4, 5, 6, 7, 8, 9, 10, 12, 13, 14, 16))
    )
    length = layer_input.shape[0]
    scale = HEAD_DIM ** (-0.5)
    inputs = layer_input.astype(jnp.float32)
    normed_one, pull_one = jax.vjp(norm_rows, inputs, gain_one, shift_one)
    act_one = normed_one.astype(jnp.bfloat16)
    bias_full = jnp.concatenate([bias_qv[0], jnp.zeros((D,), jnp.float32), bias_qv[1]])
    qkv = (jnp.dot(act_one, weight_qkv, preferred_element_type=jnp.float32) + bias_full).astype(
        jnp.bfloat16
    )
    triple = qkv.reshape(length, 3, HEADS, HEAD_DIM)
    queries = triple[:, 0]
    keys_all = triple[:, 1]
    values_all = triple[:, 2]
    attended, totals = attend_forward(queries, keys_all, values_all, scale)
    mixed = (attended * head_gain[:, None]).reshape(length, D).astype(jnp.bfloat16)
    branch = jnp.dot(mixed, weight_out, preferred_element_type=jnp.float32) + bias_out
    normed_two, pull_two = jax.vjp(norm_rows, branch, gain_two, shift_two)
    middle = inputs + normed_two
    normed_three, pull_three = jax.vjp(norm_rows, middle, gain_three, shift_three)
    act_three = normed_three.astype(jnp.bfloat16)
    hidden = jnp.dot(act_three, weight_up, preferred_element_type=jnp.float32) + bias_up
    normed_four, pull_four = jax.vjp(ffn_middle, hidden, gain_four, shift_four)
    act_four = normed_four.astype(jnp.bfloat16)
    result = middle + (
        jnp.dot(act_four, weight_down, preferred_element_type=jnp.float32) + bias_down
    )
    output = result.astype(jnp.bfloat16)
    again = (
        lax.all_gather(low_qkv, "shard", axis=0, tiled=True),
        lax.all_gather(low_out, "shard", axis=0, tiled=True),
        lax.all_gather(low_heads, "shard", axis=0, tiled=True),
        lax.all_gather(low_up, "shard", axis=0, tiled=True),
        lax.all_gather(low_down, "shard", axis=0, tiled=True),
    )
    back_qkv, back_out, back_up, back_down = (again[0], again[1], again[3], again[4])
    back_heads = again[2].astype(jnp.float32)
    cot_full = cotangent.astype(jnp.float32)
    grad_down_bias = jnp.sum(cot_full, axis=0)
    grad_down = jnp.einsum("tf,td->fd", act_four, cotangent, preferred_element_type=jnp.float32)
    grad_four = jnp.einsum("td,fd->tf", cotangent, back_down, preferred_element_type=jnp.float32)
    grad_hidden, grad_gain_four, grad_shift_four = pull_four(grad_four)
    hidden_low = grad_hidden.astype(jnp.bfloat16)
    grad_up_bias = jnp.sum(hidden_low, axis=0, dtype=jnp.float32)
    grad_up = jnp.einsum("td,tf->df", act_three, hidden_low, preferred_element_type=jnp.float32)
    grad_three = jnp.einsum("tf,df->td", hidden_low, back_up, preferred_element_type=jnp.float32)
    grad_mid_part, grad_gain_three, grad_shift_three = pull_three(grad_three)
    grad_middle = cot_full + grad_mid_part
    grad_branch, grad_gain_two, grad_shift_two = pull_two(grad_middle)
    branch_low = grad_branch.astype(jnp.bfloat16)
    grad_out_b = jnp.sum(branch_low, axis=0, dtype=jnp.float32)
    grad_out_w = jnp.einsum("td,te->de", mixed, branch_low, preferred_element_type=jnp.float32)
    grad_mixed = jnp.einsum("te,de->td", branch_low, back_out, preferred_element_type=jnp.float32)
    grad_mixed = grad_mixed.reshape(length, HEADS, HEAD_DIM)
    grad_heads = jnp.sum(grad_mixed * attended, axis=(0, 2))
    grad_attended = (grad_mixed * back_heads[:, None]).astype(jnp.bfloat16)
    grad_queries, grad_keys, grad_values = attend_backward(
        queries, keys_all, values_all, totals, grad_attended, scale
    )
    grad_qkv = (
        jnp.stack([grad_queries, grad_keys, grad_values], axis=1)
        .reshape(length, 3 * D)
        .astype(jnp.bfloat16)
    )
    grad_qv = jnp.stack(
        [
            jnp.sum(grad_qkv[:, :D], axis=0, dtype=jnp.float32),
            jnp.sum(grad_qkv[:, 2 * D :], axis=0, dtype=jnp.float32),
        ]
    )
    grad_qkv_w = jnp.einsum("td,te->de", act_one, grad_qkv, preferred_element_type=jnp.float32)
    grad_one = jnp.einsum("te,de->td", grad_qkv, back_qkv, preferred_element_type=jnp.float32)
    grad_in_part, grad_gain_one, grad_shift_one = pull_one(grad_one)
    grad_input = grad_middle + grad_in_part
    shares = (
        lax.psum_scatter(grad_qkv_w, "shard", scatter_dimension=0, tiled=True),
        lax.psum_scatter(grad_qv, "shard", scatter_dimension=1, tiled=True),
        lax.psum_scatter(grad_out_w, "shard", scatter_dimension=0, tiled=True),
        lax.psum_scatter(grad_out_b, "shard", scatter_dimension=0, tiled=True),
        lax.psum_scatter(grad_heads, "shard", scatter_dimension=0, tiled=True),
        lax.psum_scatter(grad_gain_one, "shard", scatter_dimension=0, tiled=True),
        lax.psum_scatter(grad_shift_one, "shard", scatter_dimension=0, tiled=True),
        lax.psum_scatter(grad_gain_two, "shard", scatter_dimension=0, tiled=True),
        lax.psum_scatter(grad_shift_two, "shard", scatter_dimension=0, tiled=True),
        lax.psum_scatter(grad_gain_three, "shard", scatter_dimension=0, tiled=True),
        lax.psum_scatter(grad_shift_three, "shard", scatter_dimension=0, tiled=True),
        lax.psum_scatter(grad_up, "shard", scatter_dimension=0, tiled=True),
        lax.psum_scatter(grad_up_bias, "shard", scatter_dimension=0, tiled=True),
        lax.psum_scatter(grad_gain_four, "shard", scatter_dimension=0, tiled=True),
        lax.psum_scatter(grad_shift_four, "shard", scatter_dimension=0, tiled=True),
        lax.psum_scatter(grad_down, "shard", scatter_dimension=0, tiled=True),
        lax.psum_scatter(grad_down_bias, "shard", scatter_dimension=0, tiled=True),
    )
    summed = lax.psum(
        (
            shares[0],
            shares[1],
            shares[2],
            shares[3],
            shares[4],
            shares[5],
            shares[6],
            shares[7],
            shares[8],
            shares[9],
            shares[10],
            shares[11],
            shares[12],
            shares[13],
            shares[14],
            shares[15],
            shares[16],
        ),
        "rep",
    )
    return (output, grad_input) + tuple(summed)


MESH = pl.DeviceIdType.MESH
BF16 = jnp.bfloat16
F32 = jnp.float32
UNIT_ROWS = 256
UNIT_COLS = 1024
MIB = 1 << 20
COMMS = ("d1", "d2", "z1", "z2", "z3", "u1", "w1", "u2", "w2", "u3", "w3", "g1", "g2")
SLOT = {name: index for index, name in enumerate(COMMS)}


def unit_table(dims):
    table = []
    for matrix in (3, 2, 1, 0):
        rows, cols = dims[matrix]
        for col in range(0, cols, UNIT_COLS):
            for row in range(0, rows, UNIT_ROWS):
                table.append((matrix, row, col))
    return table


def kinds_of(count):
    kinds, lines = [], 0
    for index in range(count):
        kind = "XYXYZ"[index % 5]
        if kind == "Z":
            kind = ("ZX", "ZY")[lines % 2]
            lines += 1
        kinds.append(kind)
    return kinds


def task_order(kinds):
    keys = []
    for unit, kind in enumerate(kinds):
        offsets = Z_OFFSETS if kind[0] == "Z" else XY_OFFSETS
        for step, offset in enumerate(offsets):
            keys.append((unit + offset, unit, step))
    keys.sort()
    return [(unit, step) for _, unit, step in keys]


XY_OFFSETS = (0, 3.5, 7.0, 11.5, 14.5, 17.5, 21.0, 23.0, 25.0, 27.5, 30.5)
Z_OFFSETS = (0.0, 4.5, 7.0, 10.0, 13.0, 16.5, 19.0, 23.0, 25.0, 28.0, 32.5)


GIVE_ROWS = 240


def program_order(units, kinds, costs, ends):
    steps = task_order(kinds)
    order, task, waited, left = [], 0, {3}, len(costs)
    order.append(("wait", 3, 0))
    vec_at = None
    for index, (unit, step) in enumerate(steps):
        m = units[unit][0]
        if m not in waited:
            while task < ends[m]:
                order.append(("task", task, 0))
                task += 1
            order.append(("wait", m, 0))
            waited.add(m)
        order.append(("sum", unit, step))
        if index >= 6 and task < len(costs):
            order.append(("task", task, 0))
            task += 1
            if task == len(costs):
                vec_at = {index + 6 + 8 * k: k for k in range(5)}
        if vec_at and index in vec_at:
            order.append(("vec", vec_at[index], 0))
    return order


EPS_TILE = 32


def fold(v):
    total = v[0:8]
    for k in range(1, v.shape[0] // 8):
        total = total + v[8 * k : 8 * k + 8]
    return total


def layer_kernel(dims, at_base, g_base, *refs):
    x_in, cot_in, weights, params = refs[0], refs[1], refs[2:6], refs[6:19]
    y_out, dx_out, outs, vec_out, tiles_hbm = refs[19], refs[20], refs[21:25], refs[25], refs[26]
    (
        at, g, res, give, pair, line_xy, line_z, ring, big, left, act, hid, qkv, probs, attended, branch, middle, dmid,
        vec_w, vec_h, rstd4, sums4, vec_in, vec_own, vec_got,
        send, recv, v_send, v_recv, p_send, p_recv, l_sem, o_sem, w_in, w_keep, w_send, w_recv, t_sem, s_sem, e_sem,
    ) = refs[27:]
    r = lax.axis_index("rep")
    c = lax.axis_index("shard")
    x, y, z = r % 2, (r // 2) % 2, r // 4
    core = {"shard": 1 - c}
    to = {
        "X": {"rep": r + 1 - 2 * x},
        "Y": {"rep": r + 2 - 4 * y},
        "U": {"rep": r + 4},
        "D": {"rep": r - 4},
    }
    line_end = (z == 0) | (z == 3)
    line_mid = (z == 1) | (z == 2)
    outward = {"rep": r + 4 * (2 * (z // 2) - 1)}
    inward = {"rep": r + 4 * (1 - 2 * (z // 2))}
    across = {"rep": r + 4 * (3 - 2 * z)}
    upper = z // 2
    length = x_in.shape[0]
    width = x_in.shape[1]
    half_w = width // 2
    hidden = dims[2][1]
    half_h = hidden // 2
    blocks = hidden // width
    TILE = 512

    tile_of = []
    for m, (rows, cols) in enumerate(dims):
        for row in range(0, rows, TILE):
            for col in range(0, cols, UNIT_COLS):
                tile_of.append((m, row, col))
    first_tile = [min(t for t, v in enumerate(tile_of) if v[0] == m) for m in range(4)]
    parts = 2 * len(tile_of)
    slots_f, slots_b = 6, 16

    def part_read(i):
        m, row, col = tile_of[i // 2]
        return pltpu.make_async_copy(
            weights[m].at[pl.ds(row + (i % 2) * 256, 256), pl.ds(col, UNIT_COLS)],
            big.at[pl.ds((i % slots_f) * 256, 256), :],
            w_in.at[i],
        )

    def part_low(i):
        return low_buf.at[pl.ds((i % slots_b) * 256, 256), :]

    low_buf = give

    def part_place(i):
        return tiles_hbm.at[c, i // 2, pl.ds((i % 2) * 256, 256), :]

    def part_keep(i):
        return pltpu.make_async_copy(part_low(i), part_place(i), w_keep.at[i])

    def part_give(i):
        return pltpu.make_async_remote_copy(
            src_ref=part_low(i), dst_ref=part_place(i), send_sem=w_send.at[i], recv_sem=w_recv.at[i],
            device_id=core, device_id_type=MESH,
        )

    def part_got(i):
        return pltpu.make_async_remote_copy(
            src_ref=part_low(i), dst_ref=tiles_hbm.at[1 - c, i // 2, pl.ds((i % 2) * 256, 256), :],
            send_sem=w_send.at[i], recv_sem=w_recv.at[i], device_id=core, device_id_type=MESH,
        )

    for i in range(slots_f):
        part_read(i).start()

    barrier = pltpu.get_barrier_semaphore()
    for peer in (core, to["X"], to["Y"]):
        pl.semaphore_signal(barrier, inc=1, device_id=peer, device_id_type=MESH)

    @pl.when(z < 3)
    def _():
        pl.semaphore_signal(barrier, inc=1, device_id=to["U"], device_id_type=MESH)

    @pl.when(z > 0)
    def _():
        pl.semaphore_signal(barrier, inc=1, device_id=to["D"], device_id_type=MESH)

    @pl.when(line_end)
    def _():
        pl.semaphore_signal(barrier, inc=1, device_id=across, device_id_type=MESH)

    narrow = (0, 0, 2, 3, 4, 5, 6, 7, 8, 9, 10)

    def rounded(v):
        return v.astype(BF16).astype(F32)

    lane_w = pl.ds(pl.multiple_of(c * half_w, half_w), half_w)
    lane_h = pl.ds(pl.multiple_of(c * half_h, half_h), half_h)
    (qv_ref, ob_ref, hs_ref, g1_ref, b1_ref, g2_ref, b2_ref, g3_ref, b3_ref, ub_ref, g4_ref, b4_ref, db_ref) = params
    vec_w[0:2, lane_w] = rounded(qv_ref[...])
    for row, ref in zip(range(2, 11), (ob_ref, hs_ref, g1_ref, b1_ref, g2_ref, b2_ref, g3_ref, b3_ref, db_ref)):
        vec_w[row : row + 1, lane_w] = rounded(ref[...])
    for row, ref in enumerate((ub_ref, g4_ref, b4_ref)):
        vec_h[row : row + 1, lane_h] = rounded(ref[...])
    QB, VB, OB, HS, G1, B1, G2, B2, G3, B3, DB = range(11)
    UB, G4, B4 = range(3)

    def small_copy(k, give_it):
        ref, lane, far = ((vec_w, lane_w, 1 - c), (vec_h, lane_h, 1 - c))[k]
        size = half_w if k == 0 else half_h
        other = pl.ds(pl.multiple_of((1 - c) * size, size), size)
        here = ref.at[:, lane]
        return pltpu.make_async_remote_copy(
            src_ref=here, dst_ref=here if give_it else ref.at[:, other], send_sem=s_sem.at[k, 0], recv_sem=s_sem.at[k, 1],
            device_id=core, device_id_type=MESH,
        )

    e_copy = pltpu.make_async_copy(cot_in, g.at[pl.ds(0, length), pl.ds(g_base[3], width)], e_sem.at[0])
    e_copy.start()
    e_copy.wait()
    pl.semaphore_wait(barrier, 5)
    small_copy(0, True).start()
    small_copy(1, True).start()

    def left_own(m):
        rows = dims[m][0]
        return pltpu.make_async_copy(
            left.at[pl.ds(pl.multiple_of(2 * at_base[m] + c * rows, 512), rows), :],
            at.at[pl.ds(at_base[m], rows), pl.ds(0, length)],
            l_sem.at[m],
        )

    def left_far(m):
        rows = dims[m][0]
        return pltpu.make_async_remote_copy(
            src_ref=left.at[pl.ds(pl.multiple_of(2 * at_base[m] + (1 - c) * rows, 512), rows), :],
            dst_ref=at.at[pl.ds(at_base[m], rows), pl.ds(length, length)],
            send_sem=p_send.at[m, 0], recv_sem=p_recv.at[m, 0], device_id=core, device_id_type=MESH,
        )

    def right_far(m):
        cols = pl.ds(g_base[m], dims[m][1])
        return pltpu.make_async_remote_copy(
            src_ref=g.at[pl.ds(0, length), cols], dst_ref=g.at[pl.ds(length, length), cols],
            send_sem=p_send.at[m, 1], recv_sem=p_recv.at[m, 1], device_id=core, device_id_type=MESH,
        )

    right_far(3).start()

    def start_left(m):
        left_own(m).start()
        left_far(m).start()

    def wait_pair(m):
        left_own(m).wait()
        left_far(m).wait()
        right_far(m).wait()

    for i in range(parts):
        part_read(i).wait()
        if i >= slots_b:
            part_keep(i - slots_b).wait()
            part_give(i - slots_b).wait_send()

        def convert(b, _, i=i):
            rows = pl.multiple_of((i % slots_f) * 256 + b * 32, 32)
            low = pl.multiple_of((i % slots_b) * 256 + b * 32, 32)
            low_buf[pl.ds(low, 32), :] = big[pl.ds(rows, 32), :].astype(BF16)
            return 0

        lax.fori_loop(0, 8, convert, 0)
        part_keep(i).start()
        part_give(i).start()
        if i + slots_f < parts:
            part_read(i + slots_f).start()

    def tile(m, half, index):
        return (half, first_tile[m] + index)

    stream = []
    for m in (0, 1, 2):
        for index in range(dims[m][1] // UNIT_COLS):
            stream += [tile(m, 0, index), tile(m, 1, index)]
    per_half = dims[3][0] // TILE
    stream += [tile(3, h, k) for h in range(2) for k in range(per_half)]
    for m in (2, 1, 0):
        for index in range(dims[m][1] // UNIT_COLS):
            stream += [tile(m, 0, index), tile(m, 1, index)]
    slots_t = 4
    here = set()

    def tile_load(i):
        half, t = stream[i]
        return pltpu.make_async_copy(
            tiles_hbm.at[half, t], ring.at[i % slots_t], t_sem.at[i % slots_t]
        )

    def tile_start(i):
        half, t = stream[i]
        if (1, t) not in here:
            here.add((1, t))
            for k in (2 * t, 2 * t + 1):
                if k + slots_b >= parts:
                    part_keep(k).wait()
                    part_give(k).wait_send()
                part_got(k).wait_recv()
        tile_load(i).start()

    at_tile = [0]

    def next_tile():
        i = at_tile[0]
        tile_load(i).wait()
        return ring.at[i % slots_t]

    def done_tile():
        i = at_tile[0]
        if i + slots_t < len(stream):
            tile_start(i + slots_t)
        at_tile[0] = i + 1

    def mean(v):
        return jnp.sum(v, axis=-1, keepdims=True) / v.shape[-1]

    def normal(v):
        centred = v - mean(v)
        scale = lax.rsqrt(mean(centred * centred) + 1e-05)
        return centred * scale, scale

    def each(fn, step=32, init=0):
        def body(i, carry):
            return fn(pl.ds(pl.multiple_of(i * step, step), step), carry)

        return lax.fori_loop(0, length // step, body, init)

    def w_row(i):
        return vec_w[i : i + 1, :]

    def turn(source, m, block=0):
        def body(k, _):
            cols = pl.ds(pl.multiple_of(k * 256, 256), 256)
            rows = pl.ds(pl.multiple_of(2 * at_base[m] + block * width + k * 256, 256), 256)
            left[rows, :] = jnp.transpose(source[:, cols])
            return 0

        lax.fori_loop(0, width // 256, body, 0)

    NT = (((1,), (1,)), ((), ()))
    TN = (((0,), (0,)), ((), ()))

    def nt(a, b):
        return lax.dot_general(a, b, NT, preferred_element_type=F32)

    def tn(a, b):
        return lax.dot_general(a, b, TN, preferred_element_type=F32)

    def product_pair(source, write):
        first = next_tile()
        i = at_tile[0]
        at_tile[0] = i + 1
        second = next_tile()
        at_tile[0] = i

        def body(k, _):
            cols = pl.ds(pl.multiple_of(k * 256, 256), 256)
            value = jnp.dot(source[:, 0:half_w], first[:, cols], preferred_element_type=F32)
            value = value + jnp.dot(source[:, half_w:width], second[:, cols], preferred_element_type=F32)
            write(cols, value)
            return 0

        lax.fori_loop(0, UNIT_COLS // 256, body, 0)
        done_tile()
        done_tile()

    for i in range(slots_t):
        tile_start(i)
    small_copy(0, True).wait_send()
    small_copy(1, True).wait_send()
    small_copy(0, False).wait_recv()
    small_copy(1, False).wait_recv()

    def first_norm(rows, _):
        hat, _s = normal(x_in[rows, :].astype(F32))
        act[rows, :] = (hat * w_row(G1) + w_row(B1)).astype(BF16)
        return 0

    each(first_norm)
    for index in range(3):

        def put_qkv(cols, value, index=index):
            start = pl.multiple_of(index * width + cols.start, 256)
            if index == 0:
                value = value + vec_w[QB : QB + 1, cols]
            if index == 2:
                value = value + vec_w[VB : VB + 1, cols]
            qkv[:, pl.ds(start, 256)] = value.astype(BF16)

        product_pair(act, put_qkv)
    turn(act, 0)
    start_left(0)

    low_lane = lax.broadcasted_iota(jnp.int32, (length, 128), 1) < 64
    allowed = lax.broadcasted_iota(jnp.int32, (length, length), 1) <= lax.broadcasted_iota(
        jnp.int32, (length, length), 0
    )
    scale = 64 ** (-0.5)
    keep_lane = (low_lane.astype(F32).astype(BF16), jnp.logical_not(low_lane).astype(F32).astype(BF16))

    def attend(p, _):
        q = qkv[:, pl.ds(pl.multiple_of(p * 128, 128), 128)]
        k = qkv[:, pl.ds(pl.multiple_of(width + p * 128, 128), 128)]
        v = qkv[:, pl.ds(pl.multiple_of(2 * width + p * 128, 128), 128)]
        got = []
        for h in range(2):
            own = q * keep_lane[h]
            scores = jnp.where(allowed, nt(own, k) * scale, -1e30)
            top = jnp.max(scores, axis=-1, keepdims=True)
            lse = top + jnp.log(jnp.sum(jnp.exp(scores - top), axis=-1, keepdims=True))
            prob = jnp.exp(scores - lse)
            probs[2 * p + h] = prob
            got.append(jnp.dot(prob.astype(BF16), v, preferred_element_type=F32))
        cols = pl.ds(pl.multiple_of(p * 128, 128), 128)
        value = jnp.where(low_lane, got[0], got[1])
        attended[:, cols] = value
        act[:, cols] = (value * vec_w[HS : HS + 1, cols]).astype(BF16)
        return 0

    lax.fori_loop(0, width // 128, attend, 0)

    def put_branch(cols, value):
        branch[:, cols] = value + vec_w[OB : OB + 1, cols]

    product_pair(act, put_branch)
    turn(act, 1)
    start_left(1)

    def second_norm(rows, _):
        hat, _s = normal(branch[rows, :])
        mid = x_in[rows, :].astype(F32) + (hat * w_row(G2) + w_row(B2))
        middle[rows, :] = mid
        hat, _s = normal(mid)
        act[rows, :] = (hat * w_row(G3) + w_row(B3)).astype(BF16)
        return 0

    each(second_norm)
    U0, H0, D0 = 0, blocks * length, 2 * blocks * length
    for j in range(blocks):

        def put_hidden(cols, value, j=j):
            start = pl.multiple_of(j * width + cols.start, 256)
            big[U0 + j * length : U0 + (j + 1) * length, cols] = value + vec_h[UB : UB + 1, pl.ds(start, 256)]

        product_pair(act, put_hidden)
    turn(act, 2)
    start_left(2)
    root_half = 0.7071067811865476

    def near(base, start):
        return pl.ds(pl.multiple_of(base + start, 16), 16)

    def hidden_norm(rows, _):
        total = jnp.zeros((16, 1), F32)
        for j in range(blocks):
            u = big[near(U0 + j * length, rows.start), :]
            h = u * (1.0 + lax.erf(u * root_half)) * 0.5
            big[near(H0 + j * length, rows.start), :] = h
            total = total + jnp.sum(h, axis=-1, keepdims=True)
        centre = total / hidden
        total = jnp.zeros((16, 1), F32)
        for j in range(blocks):
            h = big[near(H0 + j * length, rows.start), :] - centre
            total = total + jnp.sum(h * h, axis=-1, keepdims=True)
        s = lax.rsqrt(total / hidden + 1e-05)
        rstd4[rows, :] = jnp.broadcast_to(s, (16, 128))
        for j in range(blocks):
            at_h = near(H0 + j * length, rows.start)
            hat = (big[at_h, :] - centre) * s
            big[at_h, :] = hat
            cols = slice(j * width, (j + 1) * width)
            hid[near(j * length, rows.start), :] = (
                hat * vec_h[G4 : G4 + 1, cols] + vec_h[B4 : B4 + 1, cols]
            ).astype(BF16)
        return 0

    each(hidden_norm, 16)
    for j in range(blocks):
        turn(hid.at[pl.ds(j * length, length), :], 3, j)
    start_left(3)

    tasks = []
    zeros8 = jnp.zeros((8, width), F32)
    dirs = g.at[pl.ds(0, length), :]

    def put_sum(row, value):
        line = jnp.sum(value, axis=0, keepdims=True)
        vec_in[0, row : row + 1, :] = line[:, 0:half_w]
        vec_in[1, row : row + 1, :] = line[:, half_w:width]

    def task_down(h, k):
        def run():
            w = next_tile()
            row = h * dims[3][0] + k * TILE
            j, lane = row // width, row % width
            if h == 0 and k == 0:
                y_acc[...] = middle[...] + w_row(DB)
            for n in range(TILE // 256):
                big[D0 + j * length : D0 + (j + 1) * length, lane + n * 256 : lane + (n + 1) * 256] = nt(
                    dirs[:, g_base[3] : g_base[3] + width], w[n * 256 : (n + 1) * 256, :]
                )

            def body(n, _):
                cols = pl.ds(pl.multiple_of(n * 256, 256), 256)
                y_acc[:, cols] += jnp.dot(
                    hid[j * length : (j + 1) * length, lane : lane + TILE], w[:, cols], preferred_element_type=F32
                )
                return 0

            lax.fori_loop(0, width // 256, body, 0)
            done_tile()
            if h == 1 and k == per_half - 1:
                y_out[...] = y_acc[...].astype(BF16)

        return run

    y_acc = dmid
    for h in range(2):
        for k in range(per_half):
            tasks.append((1.2, task_down(h, k)))

    def task_hidden(first, count):
        def run():
            if first == 0:
                sums4[...] = jnp.zeros_like(sums4)

                def e_sum(rows, carry):
                    return carry + fold(dirs[rows, g_base[3] : g_base[3] + width].astype(F32))

                put_sum(DB, each(e_sum, 32, zeros8))

            def body(i, _):
                at_r = pl.multiple_of(first + i * 16, 16)
                one = jnp.zeros((16, 1), F32)
                two = jnp.zeros((16, 1), F32)
                for j in range(blocks):
                    gain = vec_h[G4 : G4 + 1, j * width : (j + 1) * width]
                    d = big[near(D0 + j * length, at_r), :] * gain
                    hat = big[near(H0 + j * length, at_r), :]
                    one = one + jnp.sum(d, axis=-1, keepdims=True)
                    two = two + jnp.sum(d * hat, axis=-1, keepdims=True)
                one, two = one / hidden, two / hidden
                s = rstd4[pl.ds(at_r, 16), 0:1]
                for j in range(blocks):
                    cols = slice(j * width, (j + 1) * width)
                    da = big[near(D0 + j * length, at_r), :]
                    hat = big[near(H0 + j * length, at_r), :]
                    u = big[near(U0 + j * length, at_r), :]
                    dh = s * (da * vec_h[G4 : G4 + 1, cols] - one - hat * two)
                    slope = 0.5 * (1.0 + lax.erf(u * root_half)) + u * (jnp.exp(u * u * -0.5) * 0.3989422804014327)
                    du = (dh * slope).astype(BF16)
                    g[pl.ds(at_r, 16), g_base[2] + j * width : g_base[2] + (j + 1) * width] = du
                    sums4[0:8, cols] += fold(du.astype(F32))
                    sums4[8:16, cols] += fold(da * hat)
                    sums4[16:24, cols] += fold(da)
                return 0

            lax.fori_loop(0, count // 16, body, 0)
            if first + count == length:
                for i in range(3):
                    line = jnp.sum(sums4[8 * i : 8 * i + 8, :], axis=0, keepdims=True)
                    for n in range(hidden // half_w):
                        hh, k = divmod(n, half_h // half_w)
                        vec_in[hh, 11 + 4 * i + k : 12 + 4 * i + k, :] = line[:, n * half_w : (n + 1) * half_w]
                right_far(2).start()

        return run

    for first in range(0, length, 32):
        tasks.append((3.0, task_hidden(first, 32)))

    def add_pair(acc, index_of, cols_of, count, width_to):
        def make(index):
            def run():
                for h in range(2):
                    w = next_tile()
                    for n in range(TILE // 256):
                        cols = slice(h * half_w + n * 256, h * half_w + (n + 1) * 256)
                        value = nt(dirs[:, cols_of(index)], w[n * 256 : (n + 1) * 256, :])
                        if index == 0:
                            acc[:, cols] = value
                        else:
                            acc[:, cols] += value
                    done_tile()

            return run

        return [(1.2, make(index)) for index in range(count)]

    ends = {2: len(tasks)}
    acc = big.at[pl.ds(U0, length), :]
    tasks += add_pair(acc, None, lambda j: slice(g_base[2] + j * width, g_base[2] + (j + 1) * width), blocks, width)

    def task_norms():
        def body(rows, carry):
            s3g, s3b, s2g, s2b, sob = carry
            da = acc[rows, :]
            hat, s = normal(middle[rows, :])
            d = da * w_row(G3)
            d_mid = dirs[rows, g_base[3] : g_base[3] + width].astype(F32) + s * (d - mean(d) - hat * mean(d * hat))
            dmid[rows, :] = d_mid
            s3g, s3b = s3g + fold(da * hat), s3b + fold(da)
            hat, s = normal(branch[rows, :])
            d = d_mid * w_row(G2)
            dy = (s * (d - mean(d) - hat * mean(d * hat))).astype(BF16)
            s2g, s2b = s2g + fold(d_mid * hat), s2b + fold(d_mid)
            g[rows, g_base[1] : g_base[1] + width] = dy
            return (s3g, s3b, s2g, s2b, sob + fold(dy.astype(F32)))

        got = each(body, 16, (zeros8,) * 5)
        for row, value in zip((G3, B3, G2, B2, OB), got):
            put_sum(row, value)
        right_far(1).start()

    tasks.append((2.5, task_norms))
    ends[1] = len(tasks)
    d_mixed = big.at[pl.ds(U0 + length, length), :]
    tasks += add_pair(d_mixed, None, lambda j: slice(g_base[1], g_base[1] + width), 1, width)

    def task_heads():
        def body(rows, carry):
            d = d_mixed[rows, :]
            act[rows, :] = (d * w_row(HS)).astype(BF16)
            return carry + fold(d * attended[rows, :])

        put_sum(HS, each(body, 32, zeros8))

    tasks.append((0.6, task_heads))

    def task_attend(first, count):
        def run():
            def body(i, _):
                p = first + i
                q_cols = pl.ds(pl.multiple_of(p * 128, 128), 128)
                k_cols = pl.ds(pl.multiple_of(width + p * 128, 128), 128)
                v_cols = pl.ds(pl.multiple_of(2 * width + p * 128, 128), 128)
                q, k, v, do = qkv[:, q_cols], qkv[:, k_cols], qkv[:, v_cols], act[:, q_cols]
                dq, dk, dv = [], [], []
                for h in range(2):
                    prob = probs[2 * p + h]
                    own = do * keep_lane[h]
                    dv.append(tn(prob.astype(BF16), do))
                    dp = nt(own, v)
                    ds = prob * (dp - jnp.sum(prob * dp, axis=-1, keepdims=True))
                    ds = ds.astype(BF16)
                    dq.append(jnp.dot(ds, k, preferred_element_type=F32) * scale)
                    dk.append(tn(ds, q) * scale)
                for cols, value in ((q_cols, dq), (k_cols, dk), (v_cols, dv)):
                    low = jnp.where(low_lane, value[0], value[1]).astype(BF16)
                    g[0:length, cols] = low
                return 0

            lax.fori_loop(0, count, body, 0)
            if first + count == width // 128:

                def sums(rows, carry):
                    a, b = carry
                    return (
                        a + fold(g[rows, 0:width].astype(F32)),
                        b + fold(g[rows, 2 * width : 3 * width].astype(F32)),
                    )

                a, b = each(sums, 32, (zeros8, zeros8))
                put_sum(QB, a)
                put_sum(VB, b)
                right_far(0).start()

        return run

    for first in range(0, width // 128, 2):
        tasks.append((3.0, task_attend(first, 2)))
    ends[0] = len(tasks)
    d_first = big.at[pl.ds(U0 + 2 * length, length), :]
    tasks += add_pair(d_first, None, lambda j: slice(j * width, (j + 1) * width), 3, width)

    def task_last():
        def body(rows, carry):
            sg, sb = carry
            da = d_first[rows, :]
            hat, s = normal(x_in[rows, :].astype(F32))
            d = da * w_row(G1)
            dx_out[rows, :] = dmid[rows, :] + s * (d - mean(d) - hat * mean(d * hat))
            return (sg + fold(da * hat), sb + fold(da))

        sg, sb = each(body, 16, (zeros8, zeros8))
        put_sum(G1, sg)
        put_sum(B1, sb)
        vec_in[0, 23:24, :] = jnp.zeros((1, half_w), F32)
        vec_in[1, 23:24, :] = jnp.zeros((1, half_w), F32)
        vec_copy(0).start()

    tasks.append((1.5, task_last))

    vec_steps = (core, to["X"], to["Y"], {"rep": r + 4 * (1 - 2 * (z % 2))}, across)

    def vec_copy(step):
        source = vec_in.at[1 - c] if step == 0 else vec_own.at[step]
        return pltpu.make_async_remote_copy(
            src_ref=source, dst_ref=vec_got.at[step], send_sem=v_send.at[step], recv_sem=v_recv.at[step],
            device_id=vec_steps[step], device_id_type=MESH,
        )

    def vec_task(k):
        vec_copy(k).wait_recv()
        total = (vec_in[c] if k == 0 else vec_own[k]) + vec_got[k]
        if k < 4:
            vec_own[k + 1] = total
            vec_copy(k + 1).start()
        else:
            vec_out[...] = total

    units = unit_table(dims)
    kinds = kinds_of(len(units))
    xy_at, z_at = {}, {}
    for unit, kind in enumerate(kinds):
        (z_at if kind[0] == "Z" else xy_at)[unit] = len(z_at) if kind[0] == "Z" else len(xy_at)

    def copy(unit, name, source, dest, device):
        return functools.partial(
            pltpu.make_async_remote_copy,
            src_ref=source, dst_ref=dest, send_sem=send.at[unit, SLOT[name]], recv_sem=recv.at[unit, SLOT[name]],
            device_id=device, device_id_type=MESH,
        )

    def rows_of(unit, start, count):
        if not isinstance(start, int):
            start = pl.multiple_of(start, 16)
        return res.at[unit, pl.ds(start, count), :]

    def product(unit, start, count, dest, dest_start, got=None, got_start=0):
        m, row, col = units[unit]
        step = 128 if count % 128 == 0 else min(count, 64)

        def block(index, _):
            part, strip = index // (UNIT_COLS // 256), index % (UNIT_COLS // 256)
            cols = pl.ds(pl.multiple_of(strip * 256, 256), 256)
            value = jnp.dot(
                at[pl.ds(pl.multiple_of(at_base[m] + row + start + part * step, 16), step), :],
                g[:, pl.ds(pl.multiple_of(g_base[m] + col + strip * 256, 256), 256)],
                preferred_element_type=F32,
            )
            if got is not None:
                value = value + got[pl.ds(pl.multiple_of(got_start + part * step, 16), step), cols].astype(F32)
            dest[pl.ds(pl.multiple_of(dest_start + part * step, 16), step), cols] = value.astype(BF16)
            return 0

        lax.fori_loop(0, (count // step) * (UNIT_COLS // 256), block, 0)

    def accumulate(unit, start, count, got, got_start, dest, dest_start):
        def block(strip, _):
            cols = pl.ds(pl.multiple_of(strip * 256, 256), 256)
            value = res[unit, pl.ds(pl.multiple_of(start, 16), count), cols].astype(F32)
            value = value + got[pl.ds(pl.multiple_of(got_start, 16), count), cols].astype(F32)
            dest[pl.ds(pl.multiple_of(dest_start, 16), count), cols] = value.astype(BF16)
            return 0

        lax.fori_loop(0, UNIT_COLS // 256, block, 0)

    def gather_line(unit, base, size, level):
        up, down = "u%d" % level, "w%d" % level
        low, high = z - (level - 1), z + (level - 1)

        @pl.when((low >= 0) & (z < 3))
        def _():
            part = rows_of(unit, base + low * size, size)
            copy(unit, up, part, part, to["U"])().start()

        @pl.when((high <= 3) & (z > 0))
        def _():
            part = rows_of(unit, base + high * size, size)
            copy(unit, down, part, part, to["D"])().start()

    def gather_arrived(unit, base, size, level):
        up, down = "u%d" % level, "w%d" % level
        low, high = z - level, z + level

        @pl.when(low >= 0)
        def _():
            part = rows_of(unit, base + low * size, size)
            copy(unit, up, part, part, to["U"])().wait_recv()

        @pl.when(high <= 3)
        def _():
            part = rows_of(unit, base + high * size, size)
            copy(unit, down, part, part, to["D"])().wait_recv()

    def gather_sent(unit, base, size):
        for level in (1, 2, 3):
            up, down = "u%d" % level, "w%d" % level
            low, high = z - (level - 1), z + (level - 1)

            @pl.when((low >= 0) & (z < 3))
            def _():
                part = rows_of(unit, base + low * size, size)
                copy(unit, up, part, part, to["U"])().wait_send()

            @pl.when((high <= 3) & (z > 0))
            def _():
                part = rows_of(unit, base + high * size, size)
                copy(unit, down, part, part, to["D"])().wait_send()

    def write_out(unit):
        m, row, col = units[unit]
        return pltpu.make_async_copy(
            res.at[unit],
            outs[m].at[pl.ds(row, UNIT_ROWS), pl.ds(col, UNIT_COLS)],
            o_sem.at[unit],
        )

    def finish(unit, base, size, sent):
        write_out(unit).start()
        for name in sent[:4]:
            name().wait_send()
        pl.when(line_end)(lambda: sent[4]().wait_send())

        @pl.when(line_mid)
        def _():
            sent[5]().wait_send()
            sent[6]().wait_send()

        gather_sent(unit, base, size)

    def task_xy(unit, step):
        half, quarter, size = UNIT_ROWS // 2, UNIT_ROWS // 4, UNIT_ROWS // 16
        first, second = ("X", "Y") if kinds[unit] == "X" else ("Y", "X")
        p, q = (x, y) if kinds[unit] == "X" else (y, x)
        line, block, out, other = line_xy.at[xy_at[unit]], res.at[unit], give.at[pl.ds(unit * GIVE_ROWS, GIVE_ROWS), :], pair.at[unit]
        keep, away_half = p * half, (1 - p) * half
        base = keep + q * quarter
        away = keep + (1 - q) * quarter
        at_z = half + quarter
        d1 = copy(unit, "d1", out.at[pl.ds(0, half), :], rows_of(unit, away_half, half), to[first])
        d2 = copy(unit, "d2", out.at[pl.ds(half, quarter), :], other.at[pl.ds(0, quarter), :], to[second])
        z1 = copy(unit, "z1", out.at[pl.ds(at_z, 3 * size), :], line.at[pl.ds(0, 3 * size), :], inward)
        z2 = copy(unit, "z2", out.at[pl.ds(at_z, 2 * size), :], line.at[pl.ds(3 * size, 2 * size), :], across)
        z3 = copy(unit, "z3", out.at[pl.ds(at_z + 2 * size, size), :], line.at[pl.ds(0, size), :], outward)
        own_quarter = rows_of(unit, base, quarter)
        g2 = copy(unit, "g2", own_quarter, own_quarter, to[second])
        own_half = rows_of(unit, keep, half)
        g1 = copy(unit, "g1", own_half, own_half, to[first])
        own = base + z * size
        if step == 0:
            product(unit, away_half, half, out, 0)
            d1().start()
        elif step == 1:
            d1().wait_recv()
            product(unit, away, quarter, out, half, block, away)
            d2().start()
            product(unit, base, quarter, block, base, block, base)
        elif step == 2:
            d2().wait_recv()

            @pl.when(line_end)
            def _():
                skip = (1 - upper) * size
                accumulate(unit, base + skip, 3 * size, other, skip, out, at_z)
                z1().start()
                accumulate(unit, own, size, other, z * size, block, own)

            @pl.when(line_mid)
            def _():
                accumulate(unit, base, quarter, other, 0, block, base)

        elif step == 3:

            @pl.when(line_mid)
            def _():
                z1().wait_recv()
                accumulate(unit, base + (1 - upper) * 2 * size, 2 * size, line, (1 - upper) * size, out, at_z)
                z2().start()
                accumulate(unit, own, size, line, upper * 2 * size, block, own)

        elif step == 4:

            @pl.when(line_mid)
            def _():
                z2().wait_recv()
                accumulate(unit, base + upper * 3 * size, size, line, (3 + upper) * size, out, at_z + 2 * size)
                z3().start()
                accumulate(unit, own, size, line, (4 - upper) * size, block, own)
                gather_line(unit, base, size, 1)

        elif step == 5:

            @pl.when(line_end)
            def _():
                z3().wait_recv()
                accumulate(unit, own, size, line, 0, block, own)
                gather_line(unit, base, size, 1)

        elif step in (6, 7):
            gather_arrived(unit, base, size, step - 5)
            gather_line(unit, base, size, step - 4)
        elif step == 8:
            gather_arrived(unit, base, size, 3)
            g2().start()
        elif step == 9:
            g2().wait_recv()
            g1().start()
        else:
            g1().wait_recv()
            finish(unit, base, size, (d1, d2, g2, g1, z1, z2, z3))

    def task_z(unit, step):
        size, half, quarter = UNIT_ROWS // 4, UNIT_ROWS // 8, UNIT_ROWS // 16
        first, second = ("X", "Y") if kinds[unit] == "ZX" else ("Y", "X")
        p, q = (x, y) if kinds[unit] == "ZX" else (y, x)
        line, block, out, other = line_z.at[z_at[unit]], res.at[unit], give.at[pl.ds(unit * GIVE_ROWS, GIVE_ROWS), :], pair.at[unit]
        own = z * size
        keep, away_half = own + p * half, own + (1 - p) * half
        base, away = keep + q * quarter, keep + (1 - q) * quarter
        at_d = 3 * size
        z1 = copy(unit, "z1", out.at[pl.ds(0, 3 * size), :], line.at[pl.ds(0, 3 * size), :], inward)
        z2 = copy(unit, "z2", out.at[pl.ds(0, 2 * size), :], line.at[pl.ds(3 * size, 2 * size), :], across)
        z3 = copy(unit, "z3", out.at[pl.ds(2 * size, size), :], line.at[pl.ds(0, size), :], outward)
        d1 = copy(unit, "d1", out.at[pl.ds(at_d, half), :], other.at[pl.ds(0, half), :], to[first])
        d2 = copy(unit, "d2", out.at[pl.ds(at_d + half, quarter), :], other.at[pl.ds(half, quarter), :], to[second])
        own_quarter = rows_of(unit, base, quarter)
        g2 = copy(unit, "g2", own_quarter, own_quarter, to[second])
        own_half = rows_of(unit, keep, half)
        g1 = copy(unit, "g1", own_half, own_half, to[first])
        if step == 0:

            @pl.when(line_end)
            def _():
                product(unit, (1 - upper) * size, 3 * size, out, 0)
                z1().start()

        elif step == 1:

            @pl.when(line_mid)
            def _():
                z1().wait_recv()
                product(unit, (1 - upper) * 2 * size, 2 * size, out, 0, line, (1 - upper) * size)
                z2().start()
                product(unit, own, size, block, own, line, upper * 2 * size)

        elif step == 2:

            @pl.when(line_mid)
            def _():
                z2().wait_recv()
                product(unit, upper * 3 * size, size, out, 2 * size, line, (3 + upper) * size)
                z3().start()
                got = (4 - upper) * size
                accumulate(unit, away_half, half, line, got + (1 - p) * half, out, at_d)
                d1().start()
                accumulate(unit, keep, half, line, got + p * half, block, keep)

        elif step == 3:

            @pl.when(line_end)
            def _():
                z3().wait_recv()
                product(unit, away_half, half, out, at_d, line, (1 - p) * half)
                d1().start()
                product(unit, keep, half, block, keep, line, p * half)

        elif step == 4:
            d1().wait_recv()
            accumulate(unit, away, quarter, other, (1 - q) * quarter, out, at_d + half)
            d2().start()
            accumulate(unit, base, quarter, other, q * quarter, block, base)
        elif step == 5:
            d2().wait_recv()
            accumulate(unit, base, quarter, other, half, block, base)
            g2().start()
        elif step == 6:
            g2().wait_recv()
            g1().start()
        elif step == 7:
            g1().wait_recv()
            gather_line(unit, 0, size, 1)
        elif step in (8, 9):
            gather_arrived(unit, 0, size, step - 7)
            gather_line(unit, 0, size, step - 6)
        else:
            gather_arrived(unit, 0, size, 3)
            finish(unit, 0, size, (d1, d2, g2, g1, z1, z2, z3))


    for kind, a, b in program_order(units, kinds, [cost for cost, _ in tasks], ends):
        if kind == "task":
            tasks[a][1]()
        elif kind == "wait":
            wait_pair(a)
        elif kind == "vec":
            vec_task(a)
        elif kinds[a][0] == "Z":
            task_z(a, b)
        else:
            task_xy(a, b)
    for step in range(5):
        vec_copy(step).wait_send()
    for unit in range(len(units)):
        write_out(unit).wait()


def whole_layer(layer_input, cotangent, weights, params):
    dims = tuple(w.shape for w in weights)
    at_rows = sum(rows for rows, _ in dims)
    g_cols = sum(cols for _, cols in dims)
    at_base = [sum(rows for rows, _ in dims[:m]) for m in range(4)]
    g_base = [sum(cols for _, cols in dims[:m]) for m in range(4)]
    length, width = layer_input.shape
    hidden = dims[2][1]
    blocks = hidden // width
    units = unit_table(dims)
    kinds = kinds_of(len(units))
    n, n_z = len(units), sum(kind[0] == "Z" for kind in kinds)
    tiles = n // 2
    hbm = pl.BlockSpec(memory_space=pl.ANY)
    vmem = pl.BlockSpec(memory_space=pltpu.VMEM)
    dma = pltpu.SemaphoreType.DMA
    small = (24, width // 2)
    got = pl.pallas_call(
        functools.partial(layer_kernel, dims, at_base, g_base),
        out_shape=[jax.ShapeDtypeStruct((length, width), BF16), jax.ShapeDtypeStruct((length, width), F32)]
        + [jax.ShapeDtypeStruct(d, BF16) for d in dims]
        + [jax.ShapeDtypeStruct(small, F32), jax.ShapeDtypeStruct((2, tiles, 512, UNIT_COLS), BF16)],
        in_specs=[vmem, hbm] + [hbm] * 4 + [vmem] * 13,
        out_specs=[vmem, vmem] + [hbm] * 4 + [vmem, hbm],
        scratch_shapes=[
            pltpu.VMEM((at_rows, 2 * length), BF16),
            pltpu.VMEM((2 * length, g_cols), BF16),
            pltpu.VMEM((n, UNIT_ROWS, UNIT_COLS), BF16),
            pltpu.VMEM((n * GIVE_ROWS, UNIT_COLS), BF16),
            pltpu.VMEM((n, UNIT_ROWS // 4, UNIT_COLS), BF16),
            pltpu.VMEM((n - n_z, 5 * UNIT_ROWS // 16, UNIT_COLS), BF16),
            pltpu.VMEM((n_z, 5 * UNIT_ROWS // 4, UNIT_COLS), BF16),
            pltpu.VMEM((4, 512, UNIT_COLS), BF16),
            pltpu.VMEM((3 * blocks * length, width), F32),
            pltpu.VMEM((2 * at_rows, length), BF16),
            pltpu.VMEM((length, width), BF16),
            pltpu.VMEM((blocks * length, width), BF16),
            pltpu.VMEM((length, 3 * width), BF16),
            pltpu.VMEM((width // 64, length, length), F32),
            pltpu.VMEM((length, width), F32),
            pltpu.VMEM((length, width), F32),
            pltpu.VMEM((length, width), F32),
            pltpu.VMEM((length, width), F32),
            pltpu.VMEM((16, width), F32),
            pltpu.VMEM((8, hidden), F32),
            pltpu.VMEM((length, 128), F32),
            pltpu.VMEM((24, hidden), F32),
            pltpu.VMEM((2,) + small, F32),
            pltpu.VMEM((5,) + small, F32),
            pltpu.VMEM((5,) + small, F32),
            dma((n, len(COMMS))),
            dma((n, len(COMMS))),
            dma((5,)),
            dma((5,)),
            dma((4, 2)),
            dma((4, 2)),
            dma((4,)),
            dma((n,)),
            dma((2 * tiles,)),
            dma((2 * tiles,)),
            dma((2 * tiles,)),
            dma((2 * tiles,)),
            dma((4,)),
            dma((2, 2)),
            dma((1,)),
        ],
        compiler_params=pltpu.CompilerParams(
            collective_id=0, has_side_effects=True, vmem_limit_bytes=67043328
        ),
        name="whole_layer",
    )(layer_input, cotangent, *weights, *params)
    return got[0], got[1], got[2:6], got[6]


def on_pair_of_cores(
    layer_input, cotangent, w_qkv, qv_bias, w_out, out_bias, head_scale, ln1_gain, ln1_bias, ln2_gain, ln2_bias,
    ln3_gain, ln3_bias, w_fc1, fc1_bias, ln4_gain, ln4_bias, w_fc2, fc2_bias,
):
    params = (
        qv_bias, out_bias, jnp.repeat(head_scale, HEAD_DIM), ln1_gain, ln1_bias, ln2_gain, ln2_bias, ln3_gain, ln3_bias,
        fc1_bias, ln4_gain, ln4_bias, fc2_bias,
    )
    params = [p.reshape(-1, p.shape[-1]) for p in params]
    output, grad_input, sums, vec = whole_layer(layer_input, cotangent, (w_qkv, w_out, w_fc1, w_fc2), params)
    sums = [s.astype(jnp.float32) for s in sums]
    rows = [vec[k] for k in range(2, 11)]
    wide = [vec[11 + 4 * k : 15 + 4 * k].reshape(-1) for k in range(3)]
    heads = rows[1].reshape(-1, HEAD_DIM).sum(axis=-1)
    return (
        output, grad_input, sums[0], vec[0:2], sums[1], rows[0], heads, rows[2], rows[3], rows[4], rows[5], rows[6],
        rows[7], sums[2], wide[0], wide[1], wide[2], sums[3], rows[8],
    )


def fits_pair(mesh):
    return mesh.shape["shard"] == 2 and mesh.shape["rep"] == 16


def solution(mesh):
    return jax.shard_map(
        on_pair_of_cores if fits_pair(mesh) else on_any_mesh,
        mesh=mesh,
        in_specs=(
            P(("rep", "shard"), None),
            P(("rep", "shard"), None),
            P("shard", None),
            P(None, "shard"),
            P("shard", None),
            P("shard"),
            P("shard"),
            P("shard"),
            P("shard"),
            P("shard"),
            P("shard"),
            P("shard"),
            P("shard"),
            P("shard", None),
            P("shard"),
            P("shard"),
            P("shard"),
            P("shard", None),
            P("shard"),
        ),
        out_specs=(
            P(("rep", "shard"), None),
            P(("rep", "shard"), None),
            P("shard", None),
            P(None, "shard"),
            P("shard", None),
            P("shard"),
            P("shard"),
            P("shard"),
            P("shard"),
            P("shard"),
            P("shard"),
            P("shard"),
            P("shard"),
            P("shard", None),
            P("shard"),
            P("shard"),
            P("shard"),
            P("shard", None),
            P("shard"),
        ),
        check_vma=False,
    )
```

profile of v0, /device:TPU:0, one launch (start us, length us, event | category | flops | bytes accessed | tf_op | source)
XLA Modules:
  0.0 284.9 jit_solution(7560594944219625752)
XLA Ops:
  0.7 0.7 broadcast_in_dim.3
  1.4 0.7 reshape_reshape.3.refs_8_
  2.0 257.9 %whole_layer.1 = (bf16[128,1024]{1,0:T(8,128)(2,1)}, f32[128,1024]{1,0:T(8,128)}, bf16[512,3072]{1,0:T(8,128)(2,1)}, bf16[512,1024]{1,0:T(8,128)(2,1)}, bf16[512...) custom-call(bf16[128,1024]{1,0:T(8,128)(2,1)} %refs_0_.1, ...), custom_call_target="tpu_custom_call" | custom-call | tf_op jit(solution)/shard_map/whole_layer/pallas_call | solution.py:1281
  260.0 1.3 slice.39
  261.3 1.6 fusion
  262.8 0.8 slice_bitcast_fusion
  263.6 0.6 copy.40
  264.2 0.1 reshape_squeeze.3
  264.3 0.6 reduce_sum.9
  264.9 0.6 copy.39
  265.5 0.6 copy.38
  266.1 0.0 copy-start.1
  266.1 2.9 %convert_element_type.13 = f32[512,1024]{1,0:T(8,128)} convert(bf16[512,1024]{1,0:T(8,128)(2,1)} %get-tuple-element.30) | non-fusion elementwise | flops 524288 | bytes 3145728 | tf_op jit(solution)/shard_map/convert_element_type | solution.py:1348
  269.1 5.4 %convert_element_type.12 = f32[512,3072]{1,0:T(8,128)} convert(bf16[512,3072]{1,0:T(8,128)(2,1)} %get-tuple-element.28) | non-fusion elementwise | flops 1572864 | bytes 9437184 | tf_op jit(solution)/shard_map/convert_element_type | solution.py:1348
  274.5 0.0 copy-done.1
  274.5 0.0 copy-start
  274.5 4.5 %convert_element_type.14 = f32[512,4096]{1,0:T(8,128)} convert(bf16[512,4096]{1,0:T(8,128)(2,1)S(1)} %copy-done.1) | non-fusion elementwise | flops 2097152 | bytes 12582912 | tf_op jit(solution)/shard_map/convert_element_type | solution.py:1348
  278.9 0.0 copy-done
  279.0 0.0 copy-start.3
  279.0 0.0 copy-start.2
  279.0 4.4 %convert_element_type.15 = f32[2048,1024]{1,0:T(8,128)} convert(bf16[2048,1024]{1,0:T(8,128)(2,1)S(1)} %copy-done) | non-fusion elementwise | flops 2097152 | bytes 12582912 | tf_op jit(solution)/shard_map/convert_element_type | solution.py:1348
  283.4 0.0 copy-done.3
  283.4 0.7 copy.43
  284.1 0.0 copy-done.2
  284.1 0.8 copy.44
Async XLA Ops:
  266.1 8.3 %copy-start.1 = (bf16[512,4096]{1,0:T(8,128)(2,1)S(1)}, bf16[512,4096]{1,0:T(8,128)(2,1)}, u32[]{:S(2)}) copy-start(bf16[512,4096]{1,0:T(8,128)(2,1)} %get-tuple-element.31) | copy-start | bytes 12582916
  274.5 4.5 %copy-start = (bf16[2048,1024]{1,0:T(8,128)(2,1)S(1)}, bf16[2048,1024]{1,0:T(8,128)(2,1)}, u32[]{:S(2)}) copy-start(bf16[2048,1024]{1,0:T(8,128)(2,1)} %get-tuple-element.32) | copy-start | bytes 12582916
  279.0 4.4 %copy-start.3 = (bf16[128,1024]{1,0:T(8,128)(2,1)S(1)}, bf16[128,1024]{1,0:T(8,128)(2,1)}, u32[]{:S(2)}) copy-start(bf16[128,1024]{1,0:T(8,128)(2,1)} %get-tuple-element.64) | copy-start | bytes 786436
  279.0 5.1 %copy-start.2 = (f32[128,1024]{1,0:T(8,128)S(1)}, f32[128,1024]{1,0:T(8,128)}, u32[]{:S(2)}) copy-start(f32[128,1024]{1,0:T(8,128)} %get-tuple-element.65) | copy-start | bytes 1572868
where the time goes:
time: 285 us
  Pallas kernels  258 us (91%)
  other arithmetic  17.9 us (6%)
  local copies, waits for them, and re-layouts  8.43 us (3%)
    pallas_call x1, Pallas kernels, whole_layer(): pl.pallas_call(functools.partial(layer_kernel, dims, at_base, g_base), ou...  258 us
    convert_element_type x4, other arithmetic, on_pair_of_cores(): sums = [s.astype(jnp.float32) for s in sums]  17.2 us

commit v1 on v0

--- a/solution.py
+++ b/solution.py
@@ -279,8 +279,9 @@
 UNIT_ROWS = 256
 UNIT_COLS = 1024
 MIB = 1 << 20
-COMMS = ("d1", "d2", "z1", "z2", "z3", "u1", "w1", "u2", "w2", "u3", "w3", "g1", "g2")
-SLOT = {name: index for index, name in enumerate(COMMS)}
+SLOT = {
+    "d1": 0, "d2": 1, "z1": 2, "z3": 2, "z2": 3, "u1": 4, "w1": 4, "u2": 5, "w2": 5, "u3": 6, "w3": 6, "g1": 7, "g2": 8,
+}
 
 
 def unit_table(dims):
@@ -293,55 +294,46 @@
     return table
 
 
-def kinds_of(count):
-    kinds, lines = [], 0
-    for index in range(count):
-        kind = "XYXYZ"[index % 5]
-        if kind == "Z":
-            kind = ("ZX", "ZY")[lines % 2]
-            lines += 1
-        kinds.append(kind)
-    return kinds
-
-
-def task_order(kinds):
-    keys = []
-    for unit, kind in enumerate(kinds):
-        offsets = Z_OFFSETS if kind[0] == "Z" else XY_OFFSETS
-        for step, offset in enumerate(offsets):
-            keys.append((unit + offset, unit, step))
-    keys.sort()
-    return [(unit, step) for _, unit, step in keys]
-
-
-XY_OFFSETS = (0, 3.5, 7.0, 11.5, 14.5, 17.5, 21.0, 23.0, 25.0, 27.5, 30.5)
-Z_OFFSETS = (0.0, 4.5, 7.0, 10.0, 13.0, 16.5, 19.0, 23.0, 25.0, 28.0, 32.5)
+KINDS = (
+    "X", "ZY", "ZY", "Y", "Y", "X", "X", "ZY", "Y", "Y", "Y", "X", "X", "ZX", "X", "ZY", "X", "ZX", "Y", "Y",
+    "X", "X", "Y", "ZY",
+)
+TASK = 24
+ORDER = (
+    5, 2, 0, 6, 7, 3, 24, 24, 24, 4, 24, 5, 24, 3, 1, 24, 2, 0, 24, 4, 24, 24, 5, 0, 2, 6, 3, 7, 24, 2, 4, 24,
+    6, 5, 2, 24, 0, 7, 2, 3, 5, 24, 24, 14, 2, 12, 4, 13, 9, 6, 11, 7, 5, 3, 8, 15, 0, 24, 2, 3, 4, 10, 24, 0,
+    6, 24, 14, 9, 4, 7, 24, 5, 13, 16, 17, 12, 6, 1, 5, 24, 8, 24, 5, 11, 24, 9, 13, 7, 10, 2, 15, 3, 0, 24, 14,
+    4, 1, 24, 12, 16, 13, 24, 24, 8, 5, 7, 2, 24, 20, 11, 21, 3, 22, 0, 10, 9, 23, 1, 16, 6, 15, 4, 17, 14, 19,
+    18, 7, 9, 13, 24, 3, 0, 2, 12, 8, 6, 5, 11, 17, 10, 14, 22, 15, 4, 1, 20, 9, 6, 19, 17, 14, 12, 21, 8, 11,
+    23, 10, 16, 3, 12, 18, 13, 8, 22, 11, 7, 0, 9, 10, 14, 15, 12, 4, 8, 1, 20, 23, 22, 11, 19, 10, 16, 17, 6,
+    20, 7, 9, 19, 14, 12, 8, 18, 18, 21, 22, 21, 23, 11, 10, 16, 16, 0, 3, 15, 13, 1, 20, 7, 9, 14, 12, 8, 22,
+    19, 4, 18, 11, 6, 10, 15, 22, 17, 21, 23, 16, 13, 20, 1, 19, 18, 21, 16, 22, 9, 14, 20, 8, 12, 19, 18, 21,
+    10, 23, 13, 11, 15, 17, 1, 22, 20, 19, 18, 21, 16, 14, 13, 15, 9, 12, 23, 1, 20, 19, 18, 21, 13, 15, 8, 11,
+    17, 10, 22, 23, 1, 20, 16, 15, 21, 19, 17, 18, 23, 22, 17, 23, 20, 19, 17, 23, 21, 18,
+)
 
 
 GIVE_ROWS = 240
 
 
-def program_order(units, kinds, costs, ends):
-    steps = task_order(kinds)
-    order, task, waited, left = [], 0, {3}, len(costs)
+def program_order(units, ends):
+    order, task, waited, step = [], 0, {3}, [0] * len(units)
     order.append(("wait", 3, 0))
-    vec_at = None
-    for index, (unit, step) in enumerate(steps):
-        m = units[unit][0]
+    for entry in ORDER:
+        if entry == TASK:
+            order.append(("task", task, 0))
+            task += 1
+            continue
+        m = units[entry][0]
         if m not in waited:
-            while task < ends[m]:
-                order.append(("task", task, 0))
-                task += 1
+            assert task >= ends[m]
             order.append(("wait", m, 0))
             waited.add(m)
-        order.append(("sum", unit, step))
-        if index >= 6 and task < len(costs):
-            order.append(("task", task, 0))
-            task += 1
-            if task == len(costs):
-                vec_at = {index + 6 + 8 * k: k for k in range(5)}
-        if vec_at and index in vec_at:
-            order.append(("vec", vec_at[index], 0))
+        order.append(("sum", entry, step[entry]))
+        step[entry] += 1
+    last = max(k for k, (kind, _, _) in enumerate(order) if kind == "task")
+    for k in range(5):
+        order.insert(min(last + 7 + 9 * k, len(order)), ("vec", k, 0))
     return order
 
 
@@ -357,12 +349,12 @@
 
 def layer_kernel(dims, at_base, g_base, *refs):
     x_in, cot_in, weights, params = refs[0], refs[1], refs[2:6], refs[6:19]
-    y_out, dx_out, outs, vec_out, tiles_hbm = refs[19], refs[20], refs[21:25], refs[25], refs[26]
+    y_out, dx_out, res, vec_out, tiles_hbm = refs[19:24]
     (
-        at, g, res, give, pair, line_xy, line_z, ring, big, left, act, hid, qkv, probs, attended, branch, middle, dmid,
+        at, g, give, pair, line_xy, line_z, ring, big, left, act, hid, qkv, probs, attended, branch, middle, dmid,
         vec_w, vec_h, rstd4, sums4, vec_in, vec_own, vec_got,
-        send, recv, v_send, v_recv, p_send, p_recv, l_sem, o_sem, w_in, w_keep, w_send, w_recv, t_sem, s_sem, e_sem,
-    ) = refs[27:]
+        send, recv, v_send, v_recv, p_send, p_recv, l_sem, w_in, w_keep, w_send, w_recv, t_sem, s_sem, e_sem,
+    ) = refs[24:]
     r = lax.axis_index("rep")
     c = lax.axis_index("shard")
     x, y, z = r % 2, (r // 2) % 2, r // 4
@@ -401,7 +393,7 @@
         return pltpu.make_async_copy(
             weights[m].at[pl.ds(row + (i % 2) * 256, 256), pl.ds(col, UNIT_COLS)],
             big.at[pl.ds((i % slots_f) * 256, 256), :],
-            w_in.at[i],
+            w_in.at[i % slots_f],
         )
 
     def part_low(i):
@@ -413,18 +405,18 @@
         return tiles_hbm.at[c, i // 2, pl.ds((i % 2) * 256, 256), :]
 
     def part_keep(i):
-        return pltpu.make_async_copy(part_low(i), part_place(i), w_keep.at[i])
+        return pltpu.make_async_copy(part_low(i), part_place(i), w_keep.at[i % slots_b])
 
     def part_give(i):
         return pltpu.make_async_remote_copy(
-            src_ref=part_low(i), dst_ref=part_place(i), send_sem=w_send.at[i], recv_sem=w_recv.at[i],
+            src_ref=part_low(i), dst_ref=part_place(i), send_sem=w_send.at[i % slots_b], recv_sem=w_recv.at[i],
             device_id=core, device_id_type=MESH,
         )
 
     def part_got(i):
         return pltpu.make_async_remote_copy(
             src_ref=part_low(i), dst_ref=tiles_hbm.at[1 - c, i // 2, pl.ds((i % 2) * 256, 256), :],
-            send_sem=w_send.at[i], recv_sem=w_recv.at[i], device_id=core, device_id_type=MESH,
+            send_sem=w_send.at[i % slots_b], recv_sem=w_recv.at[i], device_id=core, device_id_type=MESH,
         )
 
     for i in range(slots_f):
@@ -975,7 +967,7 @@
             vec_out[...] = total
 
     units = unit_table(dims)
-    kinds = kinds_of(len(units))
+    kinds = KINDS
     xy_at, z_at = {}, {}
     for unit, kind in enumerate(kinds):
         (z_at if kind[0] == "Z" else xy_at)[unit] = len(z_at) if kind[0] == "Z" else len(xy_at)
@@ -983,7 +975,7 @@
     def copy(unit, name, source, dest, device):
         return functools.partial(
             pltpu.make_async_remote_copy,
-            src_ref=source, dst_ref=dest, send_sem=send.at[unit, SLOT[name]], recv_sem=recv.at[unit, SLOT[name]],
+            src_ref=source, dst_ref=dest, send_sem=send.at[unit], recv_sem=recv.at[unit, SLOT[name]],
             device_id=device, device_id_type=MESH,
         )
 
@@ -1036,54 +1028,24 @@
             copy(unit, down, part, part, to["D"])().start()
 
     def gather_arrived(unit, base, size, level):
-        up, down = "u%d" % level, "w%d" % level
-        low, high = z - level, z + level
-
-        @pl.when(low >= 0)
-        def _():
-            part = rows_of(unit, base + low * size, size)
-            copy(unit, up, part, part, to["U"])().wait_recv()
-
-        @pl.when(high <= 3)
-        def _():
-            part = rows_of(unit, base + high * size, size)
-            copy(unit, down, part, part, to["D"])().wait_recv()
-
-    def gather_sent(unit, base, size):
-        for level in (1, 2, 3):
-            up, down = "u%d" % level, "w%d" % level
-            low, high = z - (level - 1), z + (level - 1)
-
-            @pl.when((low >= 0) & (z < 3))
-            def _():
-                part = rows_of(unit, base + low * size, size)
-                copy(unit, up, part, part, to["U"])().wait_send()
-
-            @pl.when((high <= 3) & (z > 0))
-            def _():
-                part = rows_of(unit, base + high * size, size)
-                copy(unit, down, part, part, to["D"])().wait_send()
-
-    def write_out(unit):
-        m, row, col = units[unit]
-        return pltpu.make_async_copy(
-            res.at[unit],
-            outs[m].at[pl.ds(row, UNIT_ROWS), pl.ds(col, UNIT_COLS)],
-            o_sem.at[unit],
-        )
-
-    def finish(unit, base, size, sent):
-        write_out(unit).start()
-        for name in sent[:4]:
-            name().wait_send()
-        pl.when(line_end)(lambda: sent[4]().wait_send())
-
-        @pl.when(line_mid)
-        def _():
-            sent[5]().wait_send()
-            sent[6]().wait_send()
-
-        gather_sent(unit, base, size)
+        def wait(chunks):
+            part = give.at[pl.ds(0, chunks * size), :]
+            copy(unit, "u%d" % level, part, part, to["U"])().wait_recv()
+
+        if level == 1:
+            pl.when(line_mid)(lambda: wait(2))
+        if level == 2:
+            wait(1)
+        else:
+            pl.when(line_end)(lambda: wait(1))
+
+    def finish(unit, ends, mids):
+        def wait(rows):
+            part = give.at[pl.ds(0, rows), :]
+            copy(unit, "d1", part, part, to["X"])().wait_send()
+
+        pl.when(line_end)(lambda: wait(ends))
+        pl.when(line_mid)(lambda: wait(mids))
 
     def task_xy(unit, step):
         half, quarter, size = UNIT_ROWS // 2, UNIT_ROWS // 4, UNIT_ROWS // 16
@@ -1164,7 +1126,7 @@
             g1().start()
         else:
             g1().wait_recv()
-            finish(unit, base, size, (d1, d2, g2, g1, z1, z2, z3))
+            finish(unit, 2 * half + 2 * quarter + 4 * size, 2 * half + 2 * quarter + 8 * size)
 
     def task_z(unit, step):
         size, half, quarter = UNIT_ROWS // 4, UNIT_ROWS // 8, UNIT_ROWS // 16
@@ -1241,10 +1203,10 @@
             gather_line(unit, 0, size, step - 6)
         else:
             gather_arrived(unit, 0, size, 3)
-            finish(unit, 0, size, (d1, d2, g2, g1, z1, z2, z3))
-
-
-    for kind, a, b in program_order(units, kinds, [cost for cost, _ in tasks], ends):
+            finish(unit, 2 * half + 2 * quarter + 4 * size, 2 * half + 2 * quarter + 8 * size)
+
+
+    for kind, a, b in program_order(units, ends):
         if kind == "task":
             tasks[a][1]()
         elif kind == "wait":
@@ -1257,8 +1219,6 @@
             task_xy(a, b)
     for step in range(5):
         vec_copy(step).wait_send()
-    for unit in range(len(units)):
-        write_out(unit).wait()
 
 
 def whole_layer(layer_input, cotangent, weights, params):
@@ -1271,7 +1231,7 @@
     hidden = dims[2][1]
     blocks = hidden // width
     units = unit_table(dims)
-    kinds = kinds_of(len(units))
+    kinds = KINDS
     n, n_z = len(units), sum(kind[0] == "Z" for kind in kinds)
     tiles = n // 2
     hbm = pl.BlockSpec(memory_space=pl.ANY)
@@ -1280,15 +1240,18 @@
     small = (24, width // 2)
     got = pl.pallas_call(
         functools.partial(layer_kernel, dims, at_base, g_base),
-        out_shape=[jax.ShapeDtypeStruct((length, width), BF16), jax.ShapeDtypeStruct((length, width), F32)]
-        + [jax.ShapeDtypeStruct(d, BF16) for d in dims]
-        + [jax.ShapeDtypeStruct(small, F32), jax.ShapeDtypeStruct((2, tiles, 512, UNIT_COLS), BF16)],
+        out_shape=[
+            pltpu.VMEM((length, width), BF16),
+            pltpu.VMEM((length, width), F32),
+            pltpu.VMEM((n, UNIT_ROWS, UNIT_COLS), BF16),
+            pltpu.VMEM(small, F32),
+            jax.ShapeDtypeStruct((2, tiles, 512, UNIT_COLS), BF16),
+        ],
         in_specs=[vmem, hbm] + [hbm] * 4 + [vmem] * 13,
-        out_specs=[vmem, vmem] + [hbm] * 4 + [vmem, hbm],
+        out_specs=[vmem] * 4 + [hbm],
         scratch_shapes=[
             pltpu.VMEM((at_rows, 2 * length), BF16),
             pltpu.VMEM((2 * length, g_cols), BF16),
-            pltpu.VMEM((n, UNIT_ROWS, UNIT_COLS), BF16),
             pltpu.VMEM((n * GIVE_ROWS, UNIT_COLS), BF16),
             pltpu.VMEM((n, UNIT_ROWS // 4, UNIT_COLS), BF16),
             pltpu.VMEM((n - n_z, 5 * UNIT_ROWS // 16, UNIT_COLS), BF16),
@@ -1311,28 +1274,90 @@
             pltpu.VMEM((2,) + small, F32),
             pltpu.VMEM((5,) + small, F32),
             pltpu.VMEM((5,) + small, F32),
-            dma((n, len(COMMS))),
-            dma((n, len(COMMS))),
+            dma((n,)),
+            dma((n, 9)),
             dma((5,)),
             dma((5,)),
             dma((4, 2)),
             dma((4, 2)),
             dma((4,)),
-            dma((n,)),
-            dma((2 * tiles,)),
-            dma((2 * tiles,)),
-            dma((2 * tiles,)),
+            dma((6,)),
+            dma((16,)),
+            dma((16,)),
             dma((2 * tiles,)),
             dma((4,)),
             dma((2, 2)),
             dma((1,)),
         ],
         compiler_params=pltpu.CompilerParams(
-            collective_id=0, has_side_effects=True, vmem_limit_bytes=67043328
+            collective_id=0, has_side_effects=True, vmem_limit_bytes=50 * MIB
         ),
         name="whole_layer",
     )(layer_input, cotangent, *weights, *params)
-    return got[0], got[1], got[2:6], got[6]
+    return got[:4]
+
+
+def finish_kernel(dims, *refs):
+    y_in, dx_in, res, vec = refs[0:4]
+    y_out, dx_out, outs, smalls = refs[4], refs[5], refs[6:10], refs[10:23]
+    wide, lines, o_sem, s_sem = refs[23], refs[24:37], refs[37], refs[38]
+    slots = wide.shape[0]
+    copies = [pltpu.make_async_copy(y_in, y_out, s_sem.at[13]), pltpu.make_async_copy(dx_in, dx_out, s_sem.at[14])]
+    rows_of = [range(0, 2)] + [range(k, k + 1) for k in range(2, 11)] + [range(11 + 4 * k, 15 + 4 * k) for k in range(3)]
+    for k, rows in enumerate(rows_of):
+        if len(rows) == 4:
+            for j, row in enumerate(rows):
+                lines[k][:, j * vec.shape[1] : (j + 1) * vec.shape[1]] = vec[row : row + 1, :]
+        else:
+            lines[k][...] = vec[rows.start : rows.stop, :]
+        copies.append(pltpu.make_async_copy(lines[k], smalls[k], s_sem.at[k]))
+    for piece in copies:
+        piece.start()
+    units = unit_table(dims)
+
+    def put(unit):
+        m, row, col = units[unit]
+        return pltpu.make_async_copy(
+            wide.at[unit % slots], outs[m].at[pl.ds(row, UNIT_ROWS), pl.ds(col, UNIT_COLS)], o_sem.at[unit % slots]
+        )
+
+    for unit in range(len(units)):
+        if unit >= slots:
+            put(unit - slots).wait()
+
+        def widen(b, _, unit=unit):
+            rows = pl.ds(pl.multiple_of(b * 32, 32), 32)
+            wide[unit % slots, rows, :] = res[unit, rows, :].astype(F32)
+            return 0
+
+        lax.fori_loop(0, UNIT_ROWS // 32, widen, 0)
+        put(unit).start()
+    for unit in range(len(units) - slots, len(units)):
+        put(unit).wait()
+    for piece in copies:
+        piece.wait()
+
+
+def write_results(got, dims):
+    y, dx, _, vec = got
+    half = vec.shape[1]
+    small = [(2, half)] + [(1, half)] * 9 + [(1, 4 * half)] * 3
+    hbm = pl.BlockSpec(memory_space=pl.ANY)
+    vmem = pl.BlockSpec(memory_space=pltpu.VMEM)
+    dma = pltpu.SemaphoreType.DMA
+    return pl.pallas_call(
+        functools.partial(finish_kernel, dims),
+        out_shape=[jax.ShapeDtypeStruct(y.shape, BF16), jax.ShapeDtypeStruct(dx.shape, F32)]
+        + [jax.ShapeDtypeStruct(d, F32) for d in dims]
+        + [jax.ShapeDtypeStruct(s, F32) for s in small],
+        in_specs=[vmem] * 4,
+        out_specs=[hbm] * 19,
+        scratch_shapes=[pltpu.VMEM((6, UNIT_ROWS, UNIT_COLS), F32)]
+        + [pltpu.VMEM(s, F32) for s in small]
+        + [dma((6,)), dma((15,))],
+        compiler_params=pltpu.CompilerParams(vmem_limit_bytes=30 * MIB),
+        name="write_results",
+    )(*got)
 
 
 def on_pair_of_cores(
@@ -1344,14 +1369,14 @@
         fc1_bias, ln4_gain, ln4_bias, fc2_bias,
     )
     params = [p.reshape(-1, p.shape[-1]) for p in params]
-    output, grad_input, sums, vec = whole_layer(layer_input, cotangent, (w_qkv, w_out, w_fc1, w_fc2), params)
-    sums = [s.astype(jnp.float32) for s in sums]
-    rows = [vec[k] for k in range(2, 11)]
-    wide = [vec[11 + 4 * k : 15 + 4 * k].reshape(-1) for k in range(3)]
-    heads = rows[1].reshape(-1, HEAD_DIM).sum(axis=-1)
+    weights = (w_qkv, w_out, w_fc1, w_fc2)
+    got = whole_layer(layer_input, cotangent, weights, params)
+    output, grad_input, qkv, out, up, down, *smalls = write_results(got, tuple(w.shape for w in weights))
+    heads = smalls[2].reshape(-1, HEAD_DIM).sum(axis=-1)
+    rows = [s.reshape(-1) for s in smalls]
     return (
-        output, grad_input, sums[0], vec[0:2], sums[1], rows[0], heads, rows[2], rows[3], rows[4], rows[5], rows[6],
-        rows[7], sums[2], wide[0], wide[1], wide[2], sums[3], rows[8],
+        output, grad_input, qkv, smalls[0], out, rows[1], heads, rows[3], rows[4], rows[5], rows[6], rows[7], rows[8], up,
+        rows[10], rows[11], rows[12], down, rows[9],
     )
 
 

time: 285 us -> 244 us (0.86)
  Pallas kernels: 258 us -> 240 us
  other arithmetic: 17.9 us -> 1.29 us
  local copies, waits for them, and re-layouts: 8.43 us -> 1.97 us
    pallas_call x1, Pallas kernels: 258 us -> 231 us  [whole_layer(): pl.pallas_call(functools.partial(layer_kernel, dims, at_base, g_base), ou...]
    convert_element_type x4 -> x0, other arithmetic: 17.2 us -> none  [on_pair_of_cores(): sums = [s.astype(jnp.float32) for s in sums]]
    pallas_call x0 -> x1, Pallas kernels: none -> 8.86 us  [write_results(): pl.pallas_call(functools.partial(finish_kernel, dims), out_shape=[jax.Sha...]
    unnamed x14 -> x0, local copies, waits for them, and re-layouts: 4.11 us -> none
    slice x2 -> x0, local copies, waits for them, and re-layouts: 2.86 us -> none  [the longest x1 1.55 us: on_pair_of_cores(): rows = [vec[k] for k in range(2, 11)]]
where the time goes in v1:
time: 244 us
  Pallas kernels  240 us (98%)
    pallas_call x1, Pallas kernels, whole_layer(): pl.pallas_call(functools.partial(layer_kernel, dims, at_base, g_base), ou...  231 us
    pallas_call x1, Pallas kernels, write_results(): pl.pallas_call(functools.partial(finish_kernel, dims), out_shape=[jax.Sha...  8.86 us

profile of v1, /device:TPU:0, one launch (start us, length us, event | category | flops | bytes accessed | tf_op | source)
XLA Modules:
  0.0 243.7 jit_solution(6111492394948783984)
XLA Ops:
  0.7 0.7 broadcast_in_dim.3
  1.4 0.7 reshape_reshape.3.refs_8_
  2.0 230.9 %whole_layer.1 = (bf16[128,1024]{1,0:T(8,128)(2,1)S(1)}, f32[128,1024]{1,0:T(8,128)S(1)}, bf16[24,256,1024]{2,1,0:T(8,128)(2,1)S(1)}, f32[24,512]{1,0:T(8,128)S(1)}, bf16[2,12,512,1024]{3,2,1,0:T(8,128)(2,1)}) custom-call(bf16[128,1024]{1,0:T(8,128)(2,1)} %refs_0_.1, bf16[128,1024]{1,0:T(8,128)(2,1)} %refs_1_.1, f32[512,3072]{1,0:T(8,128)} %refs_2_.1, ...), custom_call_target="tpu_custom_call" | custom-call | tf_op jit(solution)/shard_map/whole_layer/pallas_call | solution.py:1241
  232.9 8.9 %write_results.1 = (bf16[128,1024]{1,0:T(8,128)(2,1)}, f32[128,1024]{1,0:T(8,128)}, f32[512,3072]{1,0:T(8,128)}, f32[512,1024]{1,0:T(8,128)}, f32[512,4096]{1,0:...) custom-call(bf16[128,1024]{1,0:T(8,128)(2,1)S(1)} %get-tuple-element, ...), custom_call_target="tpu_custom_call" | custom-call | tf_op jit(solution)/shard_map/write_results/pallas_call | solution.py:1348
  241.8 0.5 broadcast.3
  242.3 0.7 reduce.3
  242.9 0.1 reshape.119
  243.0 0.6 reduce_sum.9

commit v2 on v1

--- a/solution.py
+++ b/solution.py
@@ -295,21 +295,21 @@
 
 
 KINDS = (
-    "X", "ZY", "ZY", "Y", "Y", "X", "X", "ZY", "Y", "Y", "Y", "X", "X", "ZX", "X", "ZY", "X", "ZX", "Y", "Y",
-    "X", "X", "Y", "ZY",
+    "X", "ZY", "ZY", "Y", "X", "Y", "X", "Y", "ZY", "X", "Y", "Y", "X", "Y", "ZY", "X", "ZY", "X", "X", "Y",
+    "X", "Y", "X", "ZY",
 )
-TASK = 24
+TASK, VECTORS = 24, 25
 ORDER = (
-    5, 2, 0, 6, 7, 3, 24, 24, 24, 4, 24, 5, 24, 3, 1, 24, 2, 0, 24, 4, 24, 24, 5, 0, 2, 6, 3, 7, 24, 2, 4, 24,
-    6, 5, 2, 24, 0, 7, 2, 3, 5, 24, 24, 14, 2, 12, 4, 13, 9, 6, 11, 7, 5, 3, 8, 15, 0, 24, 2, 3, 4, 10, 24, 0,
-    6, 24, 14, 9, 4, 7, 24, 5, 13, 16, 17, 12, 6, 1, 5, 24, 8, 24, 5, 11, 24, 9, 13, 7, 10, 2, 15, 3, 0, 24, 14,
-    4, 1, 24, 12, 16, 13, 24, 24, 8, 5, 7, 2, 24, 20, 11, 21, 3, 22, 0, 10, 9, 23, 1, 16, 6, 15, 4, 17, 14, 19,
-    18, 7, 9, 13, 24, 3, 0, 2, 12, 8, 6, 5, 11, 17, 10, 14, 22, 15, 4, 1, 20, 9, 6, 19, 17, 14, 12, 21, 8, 11,
-    23, 10, 16, 3, 12, 18, 13, 8, 22, 11, 7, 0, 9, 10, 14, 15, 12, 4, 8, 1, 20, 23, 22, 11, 19, 10, 16, 17, 6,
-    20, 7, 9, 19, 14, 12, 8, 18, 18, 21, 22, 21, 23, 11, 10, 16, 16, 0, 3, 15, 13, 1, 20, 7, 9, 14, 12, 8, 22,
-    19, 4, 18, 11, 6, 10, 15, 22, 17, 21, 23, 16, 13, 20, 1, 19, 18, 21, 16, 22, 9, 14, 20, 8, 12, 19, 18, 21,
-    10, 23, 13, 11, 15, 17, 1, 22, 20, 19, 18, 21, 16, 14, 13, 15, 9, 12, 23, 1, 20, 19, 18, 21, 13, 15, 8, 11,
-    17, 10, 22, 23, 1, 20, 16, 15, 21, 19, 17, 18, 23, 22, 17, 23, 20, 19, 17, 23, 21, 18,
+    0, 7, 1, 6, 24, 24, 24, 24, 5, 24, 24, 24, 24, 24, 2, 3, 4, 24, 24, 24, 24, 7, 1, 24, 0, 9, 14, 24, 6, 5, 4,
+    10, 24, 24, 2, 0, 24, 7, 24, 3, 17, 4, 11, 24, 14, 24, 15, 3, 5, 8, 9, 1, 10, 24, 4, 6, 24, 7, 3, 17, 0, 11,
+    1, 21, 2, 4, 12, 14, 5, 0, 7, 15, 8, 1, 10, 11, 24, 9, 17, 3, 2, 13, 18, 5, 11, 0, 4, 14, 21, 24, 20, 7, 8,
+    5, 24, 15, 3, 6, 11, 17, 9, 7, 16, 1, 6, 4, 19, 2, 15, 3, 17, 14, 13, 12, 5, 6, 17, 9, 4, 7, 11, 0, 18, 22,
+    15, 14, 5, 1, 7, 4, 10, 0, 9, 8, 17, 15, 6, 23, 16, 0, 3, 11, 2, 6, 24, 10, 15, 1, 22, 19, 9, 21, 12, 3, 18,
+    16, 20, 6, 23, 11, 4, 1, 15, 8, 13, 17, 25, 9, 14, 7, 10, 19, 2, 20, 21, 11, 23, 18, 17, 10, 25, 8, 1, 6,
+    22, 21, 19, 9, 13, 23, 2, 3, 22, 10, 0, 5, 15, 12, 20, 19, 21, 13, 23, 21, 10, 16, 18, 12, 22, 12, 13, 2,
+    11, 9, 21, 18, 19, 21, 23, 16, 20, 22, 18, 19, 15, 20, 3, 5, 7, 2, 14, 13, 18, 20, 23, 22, 12, 8, 16, 19,
+    18, 19, 20, 25, 5, 13, 1, 10, 14, 17, 13, 12, 8, 22, 16, 0, 20, 25, 2, 23, 22, 8, 9, 18, 16, 12, 23, 11, 20,
+    21, 6, 14, 18, 22, 12, 19, 14, 16, 21, 16, 13, 4, 23, 20, 16, 8, 23, 15, 22, 19, 10, 25, 17, 8, 13, 12,
 )
 
 
@@ -317,12 +317,16 @@
 
 
 def program_order(units, ends):
-    order, task, waited, step = [], 0, {3}, [0] * len(units)
+    order, task, vector, waited, step = [], 0, 0, {3}, [0] * len(units)
     order.append(("wait", 3, 0))
     for entry in ORDER:
         if entry == TASK:
             order.append(("task", task, 0))
             task += 1
+            continue
+        if entry == VECTORS:
+            order.append(("vec", vector, 0))
+            vector += 1
             continue
         m = units[entry][0]
         if m not in waited:
@@ -331,13 +335,10 @@
             waited.add(m)
         order.append(("sum", entry, step[entry]))
         step[entry] += 1
-    last = max(k for k, (kind, _, _) in enumerate(order) if kind == "task")
-    for k in range(5):
-        order.insert(min(last + 7 + 9 * k, len(order)), ("vec", k, 0))
     return order
 
 
-EPS_TILE = 32
+PAIRS = 2
 
 
 def fold(v):
@@ -466,10 +467,6 @@
 
     e_copy = pltpu.make_async_copy(cot_in, g.at[pl.ds(0, length), pl.ds(g_base[3], width)], e_sem.at[0])
     e_copy.start()
-    e_copy.wait()
-    pl.semaphore_wait(barrier, 5)
-    small_copy(0, True).start()
-    small_copy(1, True).start()
 
     def left_own(m):
         rows = dims[m][0]
@@ -494,8 +491,6 @@
             send_sem=p_send.at[m, 1], recv_sem=p_recv.at[m, 1], device_id=core, device_id_type=MESH,
         )
 
-    right_far(3).start()
-
     def start_left(m):
         left_own(m).start()
         left_far(m).start()
@@ -505,23 +500,46 @@
         left_far(m).wait()
         right_far(m).wait()
 
-    for i in range(parts):
-        part_read(i).wait()
-        if i >= slots_b:
-            part_keep(i - slots_b).wait()
-            part_give(i - slots_b).wait_send()
-
-        def convert(b, _, i=i):
-            rows = pl.multiple_of((i % slots_f) * 256 + b * 32, 32)
-            low = pl.multiple_of((i % slots_b) * 256 + b * 32, 32)
-            low_buf[pl.ds(low, 32), :] = big[pl.ds(rows, 32), :].astype(BF16)
-            return 0
-
-        lax.fori_loop(0, 8, convert, 0)
-        part_keep(i).start()
-        part_give(i).start()
-        if i + slots_f < parts:
-            part_read(i + slots_f).start()
+    converted, kept_parts, given_parts = [0], set(), set()
+
+    def kept(i):
+        if i not in kept_parts:
+            kept_parts.add(i)
+            part_keep(i).wait()
+
+    def given(i):
+        if i not in given_parts:
+            given_parts.add(i)
+            part_give(i).wait_send()
+
+    def convert_parts(upto):
+        for i in range(converted[0], upto):
+            part_read(i).wait()
+            if i >= slots_b:
+                kept(i - slots_b)
+                given(i - slots_b)
+
+            def convert(b, _, i=i):
+                rows = pl.multiple_of((i % slots_f) * 256 + b * 32, 32)
+                low = pl.multiple_of((i % slots_b) * 256 + b * 32, 32)
+                low_buf[pl.ds(low, 32), :] = big[pl.ds(rows, 32), :].astype(BF16)
+                return 0
+
+            lax.fori_loop(0, 8, convert, 0)
+            part_keep(i).start()
+            if i == 0:
+                pl.semaphore_wait(barrier, 5)
+                small_copy(0, True).start()
+                small_copy(1, True).start()
+            part_give(i).start()
+            if i + slots_f < parts:
+                part_read(i + slots_f).start()
+        converted[0] = max(converted[0], upto)
+
+    convert_parts(2)
+    e_copy.wait()
+    right_far(3).start()
+    convert_parts(4)
 
     def tile(m, half, index):
         return (half, first_tile[m] + index)
@@ -548,25 +566,30 @@
         half, t = stream[i]
         if (1, t) not in here:
             here.add((1, t))
+            convert_parts(2 * t + 2)
             for k in (2 * t, 2 * t + 1):
-                if k + slots_b >= parts:
-                    part_keep(k).wait()
-                    part_give(k).wait_send()
+                kept(k)
                 part_got(k).wait_recv()
         tile_load(i).start()
 
-    at_tile = [0]
-
-    def next_tile():
-        i = at_tile[0]
+    at_tile, started, allowed_to = [0], [0], [0]
+
+    def fill(limit=None):
+        if limit is not None:
+            allowed_to[0] = limit
+        while started[0] < min(at_tile[0] + slots_t, allowed_to[0], len(stream)):
+            tile_start(started[0])
+            started[0] += 1
+
+    def next_tile(ahead=0):
+        i = at_tile[0] + ahead
+        assert i < started[0]
         tile_load(i).wait()
         return ring.at[i % slots_t]
 
-    def done_tile():
-        i = at_tile[0]
-        if i + slots_t < len(stream):
-            tile_start(i + slots_t)
-        at_tile[0] = i + 1
+    def done_tile(count=1):
+        at_tile[0] += count
+        fill()
 
     def mean(v):
         return jnp.sum(v, axis=-1, keepdims=True) / v.shape[-1]
@@ -586,13 +609,9 @@
         return vec_w[i : i + 1, :]
 
     def turn(source, m, block=0):
-        def body(k, _):
-            cols = pl.ds(pl.multiple_of(k * 256, 256), 256)
-            rows = pl.ds(pl.multiple_of(2 * at_base[m] + block * width + k * 256, 256), 256)
-            left[rows, :] = jnp.transpose(source[:, cols])
-            return 0
-
-        lax.fori_loop(0, width // 256, body, 0)
+        for k in range(width // 256):
+            row = 2 * at_base[m] + block * width + k * 256
+            left[row : row + 256, :] = jnp.transpose(source[:, k * 256 : (k + 1) * 256])
 
     NT = (((1,), (1,)), ((), ()))
     TN = (((0,), (0,)), ((), ()))
@@ -604,25 +623,14 @@
         return lax.dot_general(a, b, TN, preferred_element_type=F32)
 
     def product_pair(source, write):
-        first = next_tile()
-        i = at_tile[0]
-        at_tile[0] = i + 1
-        second = next_tile()
-        at_tile[0] = i
-
-        def body(k, _):
-            cols = pl.ds(pl.multiple_of(k * 256, 256), 256)
+        first, second = next_tile(), next_tile(1)
+        for k in range(UNIT_COLS // 256):
+            cols = slice(k * 256, (k + 1) * 256)
             value = jnp.dot(source[:, 0:half_w], first[:, cols], preferred_element_type=F32)
             value = value + jnp.dot(source[:, half_w:width], second[:, cols], preferred_element_type=F32)
             write(cols, value)
-            return 0
-
-        lax.fori_loop(0, UNIT_COLS // 256, body, 0)
-        done_tile()
-        done_tile()
-
-    for i in range(slots_t):
-        tile_start(i)
+        done_tile(2)
+
     small_copy(0, True).wait_send()
     small_copy(1, True).wait_send()
     small_copy(0, False).wait_recv()
@@ -634,19 +642,21 @@
         return 0
 
     each(first_norm)
+    fill(8)
     for index in range(3):
 
         def put_qkv(cols, value, index=index):
-            start = pl.multiple_of(index * width + cols.start, 256)
             if index == 0:
                 value = value + vec_w[QB : QB + 1, cols]
             if index == 2:
                 value = value + vec_w[VB : VB + 1, cols]
-            qkv[:, pl.ds(start, 256)] = value.astype(BF16)
+            qkv[:, index * width + cols.start : index * width + cols.stop] = value.astype(BF16)
 
         product_pair(act, put_qkv)
+        convert_parts(10 + 2 * index)
     turn(act, 0)
     start_left(0)
+    convert_parts(16)
 
     low_lane = lax.broadcasted_iota(jnp.int32, (length, 128), 1) < 64
     allowed = lax.broadcasted_iota(jnp.int32, (length, length), 1) <= lax.broadcasted_iota(
@@ -655,7 +665,7 @@
     scale = 64 ** (-0.5)
     keep_lane = (low_lane.astype(F32).astype(BF16), jnp.logical_not(low_lane).astype(F32).astype(BF16))
 
-    def attend(p, _):
+    def attend(p):
         q = qkv[:, pl.ds(pl.multiple_of(p * 128, 128), 128)]
         k = qkv[:, pl.ds(pl.multiple_of(width + p * 128, 128), 128)]
         v = qkv[:, pl.ds(pl.multiple_of(2 * width + p * 128, 128), 128)]
@@ -672,16 +682,24 @@
         value = jnp.where(low_lane, got[0], got[1])
         attended[:, cols] = value
         act[:, cols] = (value * vec_w[HS : HS + 1, cols]).astype(BF16)
+
+    def attend_some(i, _):
+        for n in range(PAIRS):
+            attend(i * PAIRS + n)
         return 0
 
-    lax.fori_loop(0, width // 128, attend, 0)
+    lax.fori_loop(0, width // 128 // PAIRS, attend_some, 0)
+    fill(10)
+    convert_parts(20)
 
     def put_branch(cols, value):
         branch[:, cols] = value + vec_w[OB : OB + 1, cols]
 
     product_pair(act, put_branch)
+    fill(16)
     turn(act, 1)
     start_left(1)
+    convert_parts(24)
 
     def second_norm(rows, _):
         hat, _s = normal(branch[rows, :])
@@ -696,8 +714,8 @@
     for j in range(blocks):
 
         def put_hidden(cols, value, j=j):
-            start = pl.multiple_of(j * width + cols.start, 256)
-            big[U0 + j * length : U0 + (j + 1) * length, cols] = value + vec_h[UB : UB + 1, pl.ds(start, 256)]
+            wide = slice(j * width + cols.start, j * width + cols.stop)
+            big[U0 + j * length : U0 + (j + 1) * length, cols] = value + vec_h[UB : UB + 1, wide]
 
         product_pair(act, put_hidden)
     turn(act, 2)
@@ -732,9 +750,12 @@
         return 0
 
     each(hidden_norm, 16)
+    fill(len(stream))
     for j in range(blocks):
         turn(hid.at[pl.ds(j * length, length), :], 3, j)
     start_left(3)
+    for i in range(parts):
+        given(i)
 
     tasks = []
     zeros8 = jnp.zeros((8, width), F32)
@@ -757,14 +778,11 @@
                     dirs[:, g_base[3] : g_base[3] + width], w[n * 256 : (n + 1) * 256, :]
                 )
 
-            def body(n, _):
-                cols = pl.ds(pl.multiple_of(n * 256, 256), 256)
+            for n in range(width // 256):
+                cols = slice(n * 256, (n + 1) * 256)
                 y_acc[:, cols] += jnp.dot(
                     hid[j * length : (j + 1) * length, lane : lane + TILE], w[:, cols], preferred_element_type=F32
                 )
-                return 0
-
-            lax.fori_loop(0, width // 256, body, 0)
             done_tile()
             if h == 1 and k == per_half - 1:
                 y_out[...] = y_acc[...].astype(BF16)
@@ -886,8 +904,7 @@
 
     def task_attend(first, count):
         def run():
-            def body(i, _):
-                p = first + i
+            def pair_of_heads(p):
                 q_cols = pl.ds(pl.multiple_of(p * 128, 128), 128)
                 k_cols = pl.ds(pl.multiple_of(width + p * 128, 128), 128)
                 v_cols = pl.ds(pl.multiple_of(2 * width + p * 128, 128), 128)
@@ -905,9 +922,9 @@
                 for cols, value in ((q_cols, dq), (k_cols, dk), (v_cols, dv)):
                     low = jnp.where(low_lane, value[0], value[1]).astype(BF16)
                     g[0:length, cols] = low
-                return 0
-
-            lax.fori_loop(0, count, body, 0)
+
+            for n in range(count):
+                pair_of_heads(first + n)
             if first + count == width // 128:
 
                 def sums(rows, carry):

time: 244 us -> 228 us (0.934)
  Pallas kernels: 240 us -> 223 us
    pallas_call x1, Pallas kernels: 231 us -> 215 us  [whole_layer(): pl.pallas_call(functools.partial(layer_kernel, dims, at_base, g_base), ou...]
where the time goes in v2:
time: 228 us; the launch traced here: 227 us
  Pallas kernels  223 us (98%)
    pallas_call x1, Pallas kernels, whole_layer(): pl.pallas_call(functools.partial(layer_kernel, dims, at_base, g_base), ou...  215 us
    pallas_call x1, Pallas kernels, write_results(): pl.pallas_call(functools.partial(finish_kernel, dims), out_shape=[jax.Sha...  8.86 us

profile of v2, /device:TPU:0, one launch (start us, length us, event | category | flops | bytes accessed | tf_op | source)
XLA Modules:
  0.0 227.3 jit_solution(4859598184990901190)
XLA Ops:
  0.7 0.7 broadcast_in_dim.3
  1.4 0.7 reshape_reshape.3.refs_8_
  2.0 214.5 %whole_layer.1 = (bf16[128,1024]{1,0:T(8,128)(2,1)S(1)}, f32[128,1024]{1,0:T(8,128)S(1)}, bf16[24,256,1024]{2,1,0:T(8,128)(2,1)S(1)}, f32[24,512]{1,0:T(8,128)S(1)}, bf16[2,12,512,1024]{3,2,1,0:T(8,128)(2,1)}) custom-call(bf16[128,1024]{1,0:T(8,128)(2,1)} %refs_0_.1, bf16[128,1024]{1,0:T(8,128)(2,1)} %refs_1_.1, f32[512,3072]{1,0:T(8,128)} %refs_2_.1, ...), custom_call_target="tpu_custom_call" | custom-call | tf_op jit(solution)/shard_map/whole_layer/pallas_call | solution.py:1258
  216.6 8.9 %write_results.1 = (bf16[128,1024]{1,0:T(8,128)(2,1)}, f32[128,1024]{1,0:T(8,128)}, f32[512,3072]{1,0:T(8,128)}, f32[512,1024]{1,0:T(8,128)}, f32[512,4096]{1,0:...) custom-call(bf16[128,1024]{1,0:T(8,128)(2,1)S(1)} %get-tuple-element, ...), custom_call_target="tpu_custom_call" | custom-call | tf_op jit(solution)/shard_map/write_results/pallas_call | solution.py:1365
  225.4 0.5 broadcast.3
  225.9 0.7 reduce.3
  226.6 0.1 reshape.119
  226.7 0.6 reduce_sum.9

commit v3 on v2

--- a/solution.py
+++ b/solution.py
@@ -353,7 +353,7 @@
     y_out, dx_out, res, vec_out, tiles_hbm = refs[19:24]
     (
         at, g, give, pair, line_xy, line_z, ring, big, left, act, hid, qkv, probs, attended, branch, middle, dmid,
-        vec_w, vec_h, rstd4, sums4, vec_in, vec_own, vec_got,
+        late_in, vec_w, vec_h, rstd4, sums4, vec_in, vec_own, vec_got,
         send, recv, v_send, v_recv, p_send, p_recv, l_sem, w_in, w_keep, w_send, w_recv, t_sem, s_sem, e_sem,
     ) = refs[24:]
     r = lax.axis_index("rep")
@@ -387,18 +387,21 @@
                 tile_of.append((m, row, col))
     first_tile = [min(t for t, v in enumerate(tile_of) if v[0] == m) for m in range(4)]
     parts = 2 * len(tile_of)
-    slots_f, slots_b = 6, 16
+    slots_f, slots_b, late, slots_l, slots_g = 6, 16, 16, 3, 7
 
     def part_read(i):
         m, row, col = tile_of[i // 2]
         return pltpu.make_async_copy(
             weights[m].at[pl.ds(row + (i % 2) * 256, 256), pl.ds(col, UNIT_COLS)],
-            big.at[pl.ds((i % slots_f) * 256, 256), :],
-            w_in.at[i % slots_f],
+            late_in.at[pl.ds((i % slots_l) * 256, 256), :] if i >= late else big.at[pl.ds((i % slots_f) * 256, 256), :],
+            w_in.at[slots_f + i % slots_l if i >= late else i % slots_f],
         )
 
+    def low_row(i):
+        return 240 * 16 + (i - late) % slots_g * 256 if i >= late else i * 256
+
     def part_low(i):
-        return low_buf.at[pl.ds((i % slots_b) * 256, 256), :]
+        return low_buf.at[pl.ds(low_row(i), 256), :]
 
     low_buf = give
 
@@ -448,8 +451,13 @@
     lane_h = pl.ds(pl.multiple_of(c * half_h, half_h), half_h)
     (qv_ref, ob_ref, hs_ref, g1_ref, b1_ref, g2_ref, b2_ref, g3_ref, b3_ref, ub_ref, g4_ref, b4_ref, db_ref) = params
     vec_w[0:2, lane_w] = rounded(qv_ref[...])
-    for row, ref in zip(range(2, 11), (ob_ref, hs_ref, g1_ref, b1_ref, g2_ref, b2_ref, g3_ref, b3_ref, db_ref)):
+    for row, ref in zip((2, 4, 5, 6, 7, 8, 9, 10), (ob_ref, g1_ref, b1_ref, g2_ref, b2_ref, g3_ref, b3_ref, db_ref)):
         vec_w[row : row + 1, lane_w] = rounded(ref[...])
+    head_of = lax.broadcasted_iota(jnp.int32, (1, half_w), 1) // 64
+    spread = jnp.zeros((1, half_w), F32)
+    for h in range(half_w // 64):
+        spread = jnp.where(head_of == h, rounded(hs_ref[0:1, h : h + 1]), spread)
+    vec_w[3:4, lane_w] = spread
     for row, ref in enumerate((ub_ref, g4_ref, b4_ref)):
         vec_h[row : row + 1, lane_h] = rounded(ref[...])
     QB, VB, OB, HS, G1, B1, G2, B2, G3, B3, DB = range(11)
@@ -517,12 +525,19 @@
             part_read(i).wait()
             if i >= slots_b:
                 kept(i - slots_b)
-                given(i - slots_b)
-
-            def convert(b, _, i=i):
-                rows = pl.multiple_of((i % slots_f) * 256 + b * 32, 32)
-                low = pl.multiple_of((i % slots_b) * 256 + b * 32, 32)
-                low_buf[pl.ds(low, 32), :] = big[pl.ds(rows, 32), :].astype(BF16)
+            if i == late:
+                for k in range(late):
+                    kept(k)
+                    given(k)
+            if i >= late + slots_g:
+                kept(i - slots_g)
+                given(i - slots_g)
+            source, first = (late_in, i % slots_l * 256) if i >= late else (big, i % slots_f * 256)
+
+            def convert(b, _, i=i, source=source, first=first):
+                rows = pl.multiple_of(first + b * 32, 32)
+                low = pl.multiple_of(low_row(i) + b * 32, 32)
+                low_buf[pl.ds(low, 32), :] = source[pl.ds(rows, 32), :].astype(BF16)
                 return 0
 
             lax.fori_loop(0, 8, convert, 0)
@@ -532,8 +547,13 @@
                 small_copy(0, True).start()
                 small_copy(1, True).start()
             part_give(i).start()
-            if i + slots_f < parts:
+            if i >= late and i + slots_l < parts:
+                part_read(i + slots_l).start()
+            if i + slots_f < late:
                 part_read(i + slots_f).start()
+            if i == late - slots_f:
+                for k in range(slots_l):
+                    part_read(late + k).start()
         converted[0] = max(converted[0], upto)
 
     convert_parts(2)
@@ -599,11 +619,11 @@
         scale = lax.rsqrt(mean(centred * centred) + 1e-05)
         return centred * scale, scale
 
-    def each(fn, step=32, init=0):
+    def each(fn, step=32, init=0, unroll=1):
         def body(i, carry):
             return fn(pl.ds(pl.multiple_of(i * step, step), step), carry)
 
-        return lax.fori_loop(0, length // step, body, init)
+        return lax.fori_loop(0, length // step, body, init, unroll=unroll)
 
     def w_row(i):
         return vec_w[i : i + 1, :]
@@ -641,7 +661,7 @@
         act[rows, :] = (hat * w_row(G1) + w_row(B1)).astype(BF16)
         return 0
 
-    each(first_norm)
+    each(first_norm, unroll=2)
     fill(8)
     for index in range(3):
 
@@ -665,21 +685,24 @@
     scale = 64 ** (-0.5)
     keep_lane = (low_lane.astype(F32).astype(BF16), jnp.logical_not(low_lane).astype(F32).astype(BF16))
 
+    def split_heads(v):
+        return jnp.concatenate([v * keep_lane[0], v * keep_lane[1]], axis=0)
+
     def attend(p):
         q = qkv[:, pl.ds(pl.multiple_of(p * 128, 128), 128)]
         k = qkv[:, pl.ds(pl.multiple_of(width + p * 128, 128), 128)]
         v = qkv[:, pl.ds(pl.multiple_of(2 * width + p * 128, 128), 128)]
+        both = nt(q, split_heads(k)) * scale
         got = []
         for h in range(2):
-            own = q * keep_lane[h]
-            scores = jnp.where(allowed, nt(own, k) * scale, -1e30)
+            scores = jnp.where(allowed, both[:, h * length : (h + 1) * length], -1e30)
             top = jnp.max(scores, axis=-1, keepdims=True)
             lse = top + jnp.log(jnp.sum(jnp.exp(scores - top), axis=-1, keepdims=True))
-            prob = jnp.exp(scores - lse)
-            probs[2 * p + h] = prob
-            got.append(jnp.dot(prob.astype(BF16), v, preferred_element_type=F32))
+            got.append(jnp.exp(scores - lse))
+        prob = jnp.concatenate(got, axis=1)
+        probs[p] = prob
+        value = jnp.dot(prob.astype(BF16), split_heads(v), preferred_element_type=F32)
         cols = pl.ds(pl.multiple_of(p * 128, 128), 128)
-        value = jnp.where(low_lane, got[0], got[1])
         attended[:, cols] = value
         act[:, cols] = (value * vec_w[HS : HS + 1, cols]).astype(BF16)
 
@@ -690,7 +713,6 @@
 
     lax.fori_loop(0, width // 128 // PAIRS, attend_some, 0)
     fill(10)
-    convert_parts(20)
 
     def put_branch(cols, value):
         branch[:, cols] = value + vec_w[OB : OB + 1, cols]
@@ -699,7 +721,6 @@
     fill(16)
     turn(act, 1)
     start_left(1)
-    convert_parts(24)
 
     def second_norm(rows, _):
         hat, _s = normal(branch[rows, :])
@@ -709,7 +730,7 @@
         act[rows, :] = (hat * w_row(G3) + w_row(B3)).astype(BF16)
         return 0
 
-    each(second_norm)
+    each(second_norm, unroll=2)
     U0, H0, D0 = 0, blocks * length, 2 * blocks * length
     for j in range(blocks):
 
@@ -750,12 +771,10 @@
         return 0
 
     each(hidden_norm, 16)
-    fill(len(stream))
     for j in range(blocks):
         turn(hid.at[pl.ds(j * length, length), :], 3, j)
     start_left(3)
-    for i in range(parts):
-        given(i)
+    convert_parts(parts)
 
     tasks = []
     zeros8 = jnp.zeros((8, width), F32)
@@ -909,19 +928,20 @@
                 k_cols = pl.ds(pl.multiple_of(width + p * 128, 128), 128)
                 v_cols = pl.ds(pl.multiple_of(2 * width + p * 128, 128), 128)
                 q, k, v, do = qkv[:, q_cols], qkv[:, k_cols], qkv[:, v_cols], act[:, q_cols]
-                dq, dk, dv = [], [], []
+                prob = probs[p]
+                dv = tn(prob.astype(BF16), do)
+                dp = nt(do, split_heads(v))
+                ds = []
                 for h in range(2):
-                    prob = probs[2 * p + h]
-                    own = do * keep_lane[h]
-                    dv.append(tn(prob.astype(BF16), do))
-                    dp = nt(own, v)
-                    ds = prob * (dp - jnp.sum(prob * dp, axis=-1, keepdims=True))
-                    ds = ds.astype(BF16)
-                    dq.append(jnp.dot(ds, k, preferred_element_type=F32) * scale)
-                    dk.append(tn(ds, q) * scale)
-                for cols, value in ((q_cols, dq), (k_cols, dk), (v_cols, dv)):
-                    low = jnp.where(low_lane, value[0], value[1]).astype(BF16)
-                    g[0:length, cols] = low
+                    own = slice(h * length, (h + 1) * length)
+                    dot = jnp.sum(prob[:, own] * dp[:, own], axis=-1, keepdims=True)
+                    ds.append(prob[:, own] * (dp[:, own] - dot))
+                ds = jnp.concatenate(ds, axis=1).astype(BF16)
+                dq = jnp.dot(ds, split_heads(k), preferred_element_type=F32) * scale
+                dk = tn(ds, q) * scale
+                g[0:length, q_cols] = dq.astype(BF16)
+                g[0:length, k_cols] = jnp.where(low_lane, dk[0:length], dk[length : 2 * length]).astype(BF16)
+                g[0:length, v_cols] = jnp.where(low_lane, dv[0:length], dv[length : 2 * length]).astype(BF16)
 
             for n in range(count):
                 pair_of_heads(first + n)
@@ -1225,9 +1245,14 @@
 
     for kind, a, b in program_order(units, ends):
         if kind == "task":
+            if a == 0:
+                fill(len(stream))
             tasks[a][1]()
         elif kind == "wait":
             wait_pair(a)
+            if a == 1:
+                for k in range(parts):
+                    given(k)
         elif kind == "vec":
             vec_task(a)
         elif kinds[a][0] == "Z":
@@ -1279,11 +1304,12 @@
             pltpu.VMEM((length, width), BF16),
             pltpu.VMEM((blocks * length, width), BF16),
             pltpu.VMEM((length, 3 * width), BF16),
-            pltpu.VMEM((width // 64, length, length), F32),
+            pltpu.VMEM((width // 128, length, 2 * length), F32),
             pltpu.VMEM((length, width), F32),
             pltpu.VMEM((length, width), F32),
             pltpu.VMEM((length, width), F32),
             pltpu.VMEM((length, width), F32),
+            pltpu.VMEM((3 * 256, UNIT_COLS), F32),
             pltpu.VMEM((16, width), F32),
             pltpu.VMEM((8, hidden), F32),
             pltpu.VMEM((length, 128), F32),
@@ -1298,7 +1324,7 @@
             dma((4, 2)),
             dma((4, 2)),
             dma((4,)),
-            dma((6,)),
+            dma((10,)),
             dma((16,)),
             dma((16,)),
             dma((2 * tiles,)),
@@ -1322,7 +1348,15 @@
     copies = [pltpu.make_async_copy(y_in, y_out, s_sem.at[13]), pltpu.make_async_copy(dx_in, dx_out, s_sem.at[14])]
     rows_of = [range(0, 2)] + [range(k, k + 1) for k in range(2, 11)] + [range(11 + 4 * k, 15 + 4 * k) for k in range(3)]
     for k, rows in enumerate(rows_of):
-        if len(rows) == 4:
+        if k == 2:
+            head_of = lax.broadcasted_iota(jnp.int32, (1, vec.shape[1]), 1) // 64
+            lane = lax.broadcasted_iota(jnp.int32, lines[k].shape, 1)
+            total = jnp.zeros(lines[k].shape, F32)
+            for h in range(vec.shape[1] // 64):
+                one = jnp.sum(jnp.where(head_of == h, vec[3:4, :], 0.0), axis=-1, keepdims=True)
+                total = jnp.where(lane == h, one, total)
+            lines[k][...] = total
+        elif len(rows) == 4:
             for j, row in enumerate(rows):
                 lines[k][:, j * vec.shape[1] : (j + 1) * vec.shape[1]] = vec[row : row + 1, :]
         else:
@@ -1358,7 +1392,7 @@
 def write_results(got, dims):
     y, dx, _, vec = got
     half = vec.shape[1]
-    small = [(2, half)] + [(1, half)] * 9 + [(1, 4 * half)] * 3
+    small = [(2, half), (1, half), (1, half // 64)] + [(1, half)] * 7 + [(1, 4 * half)] * 3
     hbm = pl.BlockSpec(memory_space=pl.ANY)
     vmem = pl.BlockSpec(memory_space=pltpu.VMEM)
     dma = pltpu.SemaphoreType.DMA
@@ -1382,17 +1416,16 @@
     ln3_gain, ln3_bias, w_fc1, fc1_bias, ln4_gain, ln4_bias, w_fc2, fc2_bias,
 ):
     params = (
-        qv_bias, out_bias, jnp.repeat(head_scale, HEAD_DIM), ln1_gain, ln1_bias, ln2_gain, ln2_bias, ln3_gain, ln3_bias,
+        qv_bias, out_bias, head_scale, ln1_gain, ln1_bias, ln2_gain, ln2_bias, ln3_gain, ln3_bias,
         fc1_bias, ln4_gain, ln4_bias, fc2_bias,
     )
     params = [p.reshape(-1, p.shape[-1]) for p in params]
     weights = (w_qkv, w_out, w_fc1, w_fc2)
     got = whole_layer(layer_input, cotangent, weights, params)
     output, grad_input, qkv, out, up, down, *smalls = write_results(got, tuple(w.shape for w in weights))
-    heads = smalls[2].reshape(-1, HEAD_DIM).sum(axis=-1)
     rows = [s.reshape(-1) for s in smalls]
     return (
-        output, grad_input, qkv, smalls[0], out, rows[1], heads, rows[3], rows[4], rows[5], rows[6], rows[7], rows[8], up,
+        output, grad_input, qkv, smalls[0], out, rows[1], rows[2], rows[3], rows[4], rows[5], rows[6], rows[7], rows[8], up,
         rows[10], rows[11], rows[12], down, rows[9],
     )
 

time: 228 us -> 222 us (0.974)
    pallas_call x1, Pallas kernels: 215 us -> 212 us  [whole_layer(): pl.pallas_call(functools.partial(layer_kernel, dims, at_base, g_base), ou...]
where the time goes in v3:
time: 222 us
  Pallas kernels  221 us (100%)
    pallas_call x1, Pallas kernels, whole_layer(): pl.pallas_call(functools.partial(layer_kernel, dims, at_base, g_base), ou...  212 us
    pallas_call x1, Pallas kernels, write_results(): pl.pallas_call(functools.partial(finish_kernel, dims), out_shape=[jax.Sha...  8.87 us

profile of v3, /device:TPU:0, one launch (start us, length us, event | category | flops | bytes accessed | tf_op | source)
XLA Modules:
  0.0 221.6 jit_solution(292611578302110182)
XLA Ops:
  0.7 211.9 %whole_layer.1 = (bf16[128,1024]{1,0:T(8,128)(2,1)S(1)}, f32[128,1024]{1,0:T(8,128)S(1)}, bf16[24,256,1024]{2,1,0:T(8,128)(2,1)S(1)}, f32[24,512]{1,0:T(8,128)S(1)}, bf16[2,12,512,1024]{3,2,1,0:T(8,128)(2,1)}) custom-call(bf16[128,1024]{1,0:T(8,128)(2,1)} %refs_0_.1, bf16[128,1024]{1,0:T(8,128)(2,1)} %refs_1_.1, f32[512,3072]{1,0:T(8,128)} %refs_2_.1, ...), custom_call_target="tpu_custom_call" | custom-call | tf_op jit(solution)/shard_map/whole_layer/pallas_call | solution.py:1283
  212.6 8.9 %write_results.1 = (bf16[128,1024]{1,0:T(8,128)(2,1)}, f32[128,1024]{1,0:T(8,128)}, f32[512,3072]{1,0:T(8,128)}, f32[512,1024]{1,0:T(8,128)}, f32[512,4096]{1,0:...) custom-call(bf16[128,1024]{1,0:T(8,128)(2,1)S(1)} %get-tuple-element, ...), custom_call_target="tpu_custom_call" | custom-call | tf_op jit(solution)/shard_map/write_results/pallas_call | solution.py:1399

commit v4 on v3

--- a/solution.py
+++ b/solution.py
@@ -295,21 +295,21 @@
 
 
 KINDS = (
-    "X", "ZY", "ZY", "Y", "X", "Y", "X", "Y", "ZY", "X", "Y", "Y", "X", "Y", "ZY", "X", "ZY", "X", "X", "Y",
-    "X", "Y", "X", "ZY",
+    "YA", "YA", "YA", "XA", "XA", "YA", "XA", "XA", "ZX", "X", "X", "X", "Y", "Y", "ZY", "ZY", "X", "Y", "X",
+    "ZY", "Y", "Y", "X", "ZX",
 )
 TASK, VECTORS = 24, 25
 ORDER = (
-    0, 7, 1, 6, 24, 24, 24, 24, 5, 24, 24, 24, 24, 24, 2, 3, 4, 24, 24, 24, 24, 7, 1, 24, 0, 9, 14, 24, 6, 5, 4,
-    10, 24, 24, 2, 0, 24, 7, 24, 3, 17, 4, 11, 24, 14, 24, 15, 3, 5, 8, 9, 1, 10, 24, 4, 6, 24, 7, 3, 17, 0, 11,
-    1, 21, 2, 4, 12, 14, 5, 0, 7, 15, 8, 1, 10, 11, 24, 9, 17, 3, 2, 13, 18, 5, 11, 0, 4, 14, 21, 24, 20, 7, 8,
-    5, 24, 15, 3, 6, 11, 17, 9, 7, 16, 1, 6, 4, 19, 2, 15, 3, 17, 14, 13, 12, 5, 6, 17, 9, 4, 7, 11, 0, 18, 22,
-    15, 14, 5, 1, 7, 4, 10, 0, 9, 8, 17, 15, 6, 23, 16, 0, 3, 11, 2, 6, 24, 10, 15, 1, 22, 19, 9, 21, 12, 3, 18,
-    16, 20, 6, 23, 11, 4, 1, 15, 8, 13, 17, 25, 9, 14, 7, 10, 19, 2, 20, 21, 11, 23, 18, 17, 10, 25, 8, 1, 6,
-    22, 21, 19, 9, 13, 23, 2, 3, 22, 10, 0, 5, 15, 12, 20, 19, 21, 13, 23, 21, 10, 16, 18, 12, 22, 12, 13, 2,
-    11, 9, 21, 18, 19, 21, 23, 16, 20, 22, 18, 19, 15, 20, 3, 5, 7, 2, 14, 13, 18, 20, 23, 22, 12, 8, 16, 19,
-    18, 19, 20, 25, 5, 13, 1, 10, 14, 17, 13, 12, 8, 22, 16, 0, 20, 25, 2, 23, 22, 8, 9, 18, 16, 12, 23, 11, 20,
-    21, 6, 14, 18, 22, 12, 19, 14, 16, 21, 16, 13, 4, 23, 20, 16, 8, 23, 15, 22, 19, 10, 25, 17, 8, 13, 12,
+    5, 7, 3, 24, 24, 2, 1, 0, 6, 24, 24, 24, 5, 24, 3, 24, 2, 24, 24, 5, 24, 24, 3, 4, 24, 0, 2, 6, 15, 5, 11,
+    14, 13, 1, 4, 24, 24, 12, 3, 9, 5, 10, 2, 24, 24, 24, 24, 24, 24, 2, 15, 16, 6, 11, 17, 24, 24, 4, 24, 6,
+    14, 3, 2, 11, 1, 7, 12, 3, 2, 20, 0, 23, 11, 6, 18, 13, 4, 9, 24, 3, 0, 11, 6, 16, 14, 5, 22, 15, 24, 21,
+    20, 19, 3, 0, 1, 14, 9, 17, 23, 6, 15, 3, 2, 0, 24, 11, 18, 1, 5, 14, 2, 10, 4, 22, 19, 6, 4, 20, 23, 21,
+    24, 1, 6, 11, 7, 4, 14, 17, 3, 5, 2, 9, 0, 10, 15, 19, 20, 13, 16, 7, 1, 14, 9, 23, 6, 17, 20, 0, 11, 15, 1,
+    10, 18, 12, 23, 13, 7, 17, 11, 0, 19, 20, 2, 16, 9, 25, 4, 13, 1, 22, 7, 20, 4, 10, 9, 21, 12, 22, 20, 17,
+    0, 10, 23, 11, 16, 13, 3, 8, 7, 12, 19, 17, 10, 16, 13, 12, 14, 18, 7, 20, 6, 9, 4, 15, 25, 17, 1, 15, 22,
+    23, 18, 10, 9, 25, 8, 17, 16, 7, 19, 10, 13, 12, 21, 5, 13, 1, 18, 15, 17, 9, 8, 20, 12, 18, 21, 22, 19, 10,
+    13, 15, 8, 22, 21, 14, 21, 25, 7, 16, 8, 14, 21, 22, 19, 16, 12, 8, 22, 21, 23, 5, 0, 8, 19, 18, 16, 23, 8,
+    18, 14, 10, 4, 21, 25, 23, 9, 12, 19, 22, 23, 20, 15, 18, 8, 19, 16, 13, 22, 11, 8, 5, 17, 21, 12, 7, 8, 18,
 )
 
 
@@ -353,8 +353,8 @@
     y_out, dx_out, res, vec_out, tiles_hbm = refs[19:24]
     (
         at, g, give, pair, line_xy, line_z, ring, big, left, act, hid, qkv, probs, attended, branch, middle, dmid,
-        late_in, vec_w, vec_h, rstd4, sums4, vec_in, vec_own, vec_got,
-        send, recv, v_send, v_recv, p_send, p_recv, l_sem, w_in, w_keep, w_send, w_recv, t_sem, s_sem, e_sem,
+        late_in, near_left, near_right, vec_w, vec_h, rstd4, sums4, vec_in, vec_own, vec_got,
+        send, recv, v_send, v_recv, p_send, p_recv, l_sem, w_in, w_keep, w_send, w_recv, t_sem, s_sem, e_sem, n_send, n_recv,
     ) = refs[24:]
     r = lax.axis_index("rep")
     c = lax.axis_index("shard")
@@ -387,7 +387,7 @@
                 tile_of.append((m, row, col))
     first_tile = [min(t for t, v in enumerate(tile_of) if v[0] == m) for m in range(4)]
     parts = 2 * len(tile_of)
-    slots_f, slots_b, late, slots_l, slots_g = 6, 16, 16, 3, 7
+    slots_f, slots_b, late, slots_l, slots_g = 6, 16, 16, 2, 7
 
     def part_read(i):
         m, row, col = tile_of[i // 2]
@@ -556,9 +556,21 @@
                     part_read(late + k).start()
         converted[0] = max(converted[0], upto)
 
+    def cotangent_copy(k, relay):
+        here, there = pl.ds(0, length), pl.ds(length, length)
+        cols = pl.ds(g_base[3], width)
+        return pltpu.make_async_remote_copy(
+            src_ref=near_right.at[k, here, :] if relay else g.at[here, cols],
+            dst_ref=near_right.at[k, there if relay else here, :],
+            send_sem=n_send.at[k, int(relay)], recv_sem=n_recv.at[k, int(relay)],
+            device_id=core if relay else to["XY"[k]], device_id_type=MESH,
+        )
+
     convert_parts(2)
     e_copy.wait()
     right_far(3).start()
+    cotangent_copy(0, False).start()
+    cotangent_copy(1, False).start()
     convert_parts(4)
 
     def tile(m, half, index):
@@ -713,6 +725,9 @@
 
     lax.fori_loop(0, width // 128 // PAIRS, attend_some, 0)
     fill(10)
+    for k in range(2):
+        cotangent_copy(k, False).wait()
+        cotangent_copy(k, True).start()
 
     def put_branch(cols, value):
         branch[:, cols] = value + vec_w[OB : OB + 1, cols]
@@ -1021,7 +1036,7 @@
             start = pl.multiple_of(start, 16)
         return res.at[unit, pl.ds(start, count), :]
 
-    def product(unit, start, count, dest, dest_start, got=None, got_start=0):
+    def product(unit, start, count, dest, dest_start, got=None, got_start=0, near=None, near_start=0):
         m, row, col = units[unit]
         step = 128 if count % 128 == 0 else min(count, 64)
 
@@ -1033,6 +1048,12 @@
                 g[:, pl.ds(pl.multiple_of(g_base[m] + col + strip * 256, 256), 256)],
                 preferred_element_type=F32,
             )
+            if near is not None:
+                value = value + jnp.dot(
+                    near_left[unit, pl.ds(pl.multiple_of(near_start + part * step, 16), step), :],
+                    near[:, pl.ds(pl.multiple_of(col + strip * 256, 256), 256)],
+                    preferred_element_type=F32,
+                )
             if got is not None:
                 value = value + got[pl.ds(pl.multiple_of(got_start + part * step, 16), step), cols].astype(F32)
             dest[pl.ds(pl.multiple_of(dest_start + part * step, 16), step), cols] = value.astype(BF16)
@@ -1086,14 +1107,20 @@
 
     def task_xy(unit, step):
         half, quarter, size = UNIT_ROWS // 2, UNIT_ROWS // 4, UNIT_ROWS // 16
-        first, second = ("X", "Y") if kinds[unit] == "X" else ("Y", "X")
-        p, q = (x, y) if kinds[unit] == "X" else (y, x)
+        first, second = ("X", "Y") if kinds[unit][0] == "X" else ("Y", "X")
+        p, q = (x, y) if kinds[unit][0] == "X" else (y, x)
+        by_tokens = kinds[unit] in ("XA", "YA")
         line, block, out, other = line_xy.at[xy_at[unit]], res.at[unit], give.at[pl.ds(unit * GIVE_ROWS, GIVE_ROWS), :], pair.at[unit]
         keep, away_half = p * half, (1 - p) * half
         base = keep + q * quarter
         away = keep + (1 - q) * quarter
         at_z = half + quarter
-        d1 = copy(unit, "d1", out.at[pl.ds(0, half), :], rows_of(unit, away_half, half), to[first])
+        if by_tokens:
+            m, row, _ = units[unit]
+            give_left = at.at[pl.ds(pl.multiple_of(at_base[m] + row + away_half, 128), half), :]
+            d1 = copy(unit, "d1", give_left, near_left.at[unit], to[first])
+        else:
+            d1 = copy(unit, "d1", out.at[pl.ds(0, half), :], rows_of(unit, away_half, half), to[first])
         d2 = copy(unit, "d2", out.at[pl.ds(half, quarter), :], other.at[pl.ds(0, quarter), :], to[second])
         z1 = copy(unit, "z1", out.at[pl.ds(at_z, 3 * size), :], line.at[pl.ds(0, 3 * size), :], inward)
         z2 = copy(unit, "z2", out.at[pl.ds(at_z, 2 * size), :], line.at[pl.ds(3 * size, 2 * size), :], across)
@@ -1103,7 +1130,15 @@
         own_half = rows_of(unit, keep, half)
         g1 = copy(unit, "g1", own_half, own_half, to[first])
         own = base + z * size
-        if step == 0:
+        if step == 0 and by_tokens:
+            d1().start()
+        elif step == 1 and by_tokens:
+            d1().wait_recv()
+            near = near_right.at["XY".index(first)]
+            product(unit, away, quarter, out, half, near=near, near_start=(1 - q) * quarter)
+            d2().start()
+            product(unit, base, quarter, block, base, near=near, near_start=q * quarter)
+        elif step == 0:
             product(unit, away_half, half, out, 0)
             d1().start()
         elif step == 1:
@@ -1163,7 +1198,8 @@
             g1().start()
         else:
             g1().wait_recv()
-            finish(unit, 2 * half + 2 * quarter + 4 * size, 2 * half + 2 * quarter + 8 * size)
+            sent = 2 * quarter + half + (half // 4 if by_tokens else half)
+            finish(unit, sent + 4 * size, sent + 8 * size)
 
     def task_z(unit, step):
         size, half, quarter = UNIT_ROWS // 4, UNIT_ROWS // 8, UNIT_ROWS // 16
@@ -1250,6 +1286,9 @@
             tasks[a][1]()
         elif kind == "wait":
             wait_pair(a)
+            if a == 3:
+                for k in range(2):
+                    cotangent_copy(k, True).wait()
             if a == 1:
                 for k in range(parts):
                     given(k)
@@ -1309,7 +1348,9 @@
             pltpu.VMEM((length, width), F32),
             pltpu.VMEM((length, width), F32),
             pltpu.VMEM((length, width), F32),
-            pltpu.VMEM((3 * 256, UNIT_COLS), F32),
+            pltpu.VMEM((2 * 256, UNIT_COLS), F32),
+            pltpu.VMEM((dims[3][0] // UNIT_ROWS, UNIT_ROWS // 2, 2 * length), BF16),
+            pltpu.VMEM((2, 2 * length, width), BF16),
             pltpu.VMEM((16, width), F32),
             pltpu.VMEM((8, hidden), F32),
             pltpu.VMEM((length, 128), F32),
@@ -1331,6 +1372,8 @@
             dma((4,)),
             dma((2, 2)),
             dma((1,)),
+            dma((2, 2)),
+            dma((2, 2)),
         ],
         compiler_params=pltpu.CompilerParams(
             collective_id=0, has_side_effects=True, vmem_limit_bytes=50 * MIB

time: 222 us -> 215 us (0.968)
  Pallas kernels: 221 us -> 214 us
    pallas_call x1, Pallas kernels: 212 us -> 205 us  [whole_layer(): pl.pallas_call(functools.partial(layer_kernel, dims, at_base, g_base), ou...]
where the time goes in v4:
time: 215 us
  Pallas kernels  214 us (100%)
    pallas_call x1, Pallas kernels, whole_layer(): pl.pallas_call(functools.partial(layer_kernel, dims, at_base, g_base), ou...  205 us
    pallas_call x1, Pallas kernels, write_results(): pl.pallas_call(functools.partial(finish_kernel, dims), out_shape=[jax.Sha...  8.87 us

profile of v4, /device:TPU:0, one launch (start us, length us, event | category | flops | bytes accessed | tf_op | source)
XLA Modules:
  0.0 215.1 jit_solution(15432262955531587981)
XLA Ops:
  0.7 205.4 %whole_layer.1 = (bf16[128,1024]{1,0:T(8,128)(2,1)S(1)}, f32[128,1024]{1,0:T(8,128)S(1)}, bf16[24,256,1024]{2,1,0:T(8,128)(2,1)S(1)}, f32[24,512]{1,0:T(8,128)S(1)}, bf16[2,12,512,1024]{3,2,1,0:T(8,128)(2,1)}) custom-call(bf16[128,1024]{1,0:T(8,128)(2,1)} %refs_0_.1, bf16[128,1024]{1,0:T(8,128)(2,1)} %refs_1_.1, f32[512,3072]{1,0:T(8,128)} %refs_2_.1, ...), custom_call_target="tpu_custom_call" | custom-call | tf_op jit(solution)/shard_map/whole_layer/pallas_call | solution.py:1322
  206.1 8.9 %write_results.1 = (bf16[128,1024]{1,0:T(8,128)(2,1)}, f32[128,1024]{1,0:T(8,128)}, f32[512,3072]{1,0:T(8,128)}, f32[512,1024]{1,0:T(8,128)}, f32[512,4096]{1,0:...) custom-call(bf16[128,1024]{1,0:T(8,128)(2,1)S(1)} %get-tuple-element, ...), custom_call_target="tpu_custom_call" | custom-call | tf_op jit(solution)/shard_map/write_results/pallas_call | solution.py:1442

commit v5 on v3

--- a/solution.py
+++ b/solution.py
@@ -295,21 +295,21 @@
 
 
 KINDS = (
-    "X", "ZY", "ZY", "Y", "X", "Y", "X", "Y", "ZY", "X", "Y", "Y", "X", "Y", "ZY", "X", "ZY", "X", "X", "Y",
-    "X", "Y", "X", "ZY",
+    "QX", "QX", "QX", "QY", "QY", "QY", "QY", "QY", "Y", "X", "X", "Y", "ZY", "ZY", "X", "Y", "X", "X", "ZY",
+    "Y", "Y", "X", "ZY", "X",
 )
 TASK, VECTORS = 24, 25
 ORDER = (
-    0, 7, 1, 6, 24, 24, 24, 24, 5, 24, 24, 24, 24, 24, 2, 3, 4, 24, 24, 24, 24, 7, 1, 24, 0, 9, 14, 24, 6, 5, 4,
-    10, 24, 24, 2, 0, 24, 7, 24, 3, 17, 4, 11, 24, 14, 24, 15, 3, 5, 8, 9, 1, 10, 24, 4, 6, 24, 7, 3, 17, 0, 11,
-    1, 21, 2, 4, 12, 14, 5, 0, 7, 15, 8, 1, 10, 11, 24, 9, 17, 3, 2, 13, 18, 5, 11, 0, 4, 14, 21, 24, 20, 7, 8,
-    5, 24, 15, 3, 6, 11, 17, 9, 7, 16, 1, 6, 4, 19, 2, 15, 3, 17, 14, 13, 12, 5, 6, 17, 9, 4, 7, 11, 0, 18, 22,
-    15, 14, 5, 1, 7, 4, 10, 0, 9, 8, 17, 15, 6, 23, 16, 0, 3, 11, 2, 6, 24, 10, 15, 1, 22, 19, 9, 21, 12, 3, 18,
-    16, 20, 6, 23, 11, 4, 1, 15, 8, 13, 17, 25, 9, 14, 7, 10, 19, 2, 20, 21, 11, 23, 18, 17, 10, 25, 8, 1, 6,
-    22, 21, 19, 9, 13, 23, 2, 3, 22, 10, 0, 5, 15, 12, 20, 19, 21, 13, 23, 21, 10, 16, 18, 12, 22, 12, 13, 2,
-    11, 9, 21, 18, 19, 21, 23, 16, 20, 22, 18, 19, 15, 20, 3, 5, 7, 2, 14, 13, 18, 20, 23, 22, 12, 8, 16, 19,
-    18, 19, 20, 25, 5, 13, 1, 10, 14, 17, 13, 12, 8, 22, 16, 0, 20, 25, 2, 23, 22, 8, 9, 18, 16, 12, 23, 11, 20,
-    21, 6, 14, 18, 22, 12, 19, 14, 16, 21, 16, 13, 4, 23, 20, 16, 8, 23, 15, 22, 19, 10, 25, 17, 8, 13, 12,
+    1, 5, 24, 2, 3, 5, 0, 24, 4, 0, 4, 24, 2, 24, 24, 1, 24, 24, 24, 24, 24, 24, 24, 6, 5, 7, 4, 10, 6, 8, 11,
+    7, 13, 2, 24, 24, 14, 15, 24, 5, 4, 24, 24, 24, 5, 0, 9, 10, 4, 16, 17, 5, 13, 7, 2, 24, 12, 24, 14, 24, 24,
+    4, 9, 7, 5, 24, 16, 6, 8, 7, 0, 3, 10, 19, 12, 20, 2, 23, 21, 5, 1, 9, 0, 5, 10, 7, 13, 0, 4, 12, 6, 1, 2,
+    2, 9, 8, 3, 23, 0, 13, 16, 17, 4, 24, 11, 16, 22, 4, 6, 12, 7, 8, 5, 13, 24, 0, 3, 21, 9, 15, 2, 6, 16, 20,
+    24, 8, 11, 13, 17, 7, 2, 16, 3, 12, 7, 22, 10, 4, 6, 15, 19, 16, 3, 11, 24, 12, 8, 8, 0, 3, 14, 15, 1, 7,
+    10, 2, 20, 22, 23, 11, 17, 10, 15, 9, 1, 19, 21, 14, 25, 18, 12, 0, 20, 3, 10, 1, 13, 16, 6, 22, 21, 3, 8,
+    19, 20, 1, 10, 22, 9, 16, 23, 21, 6, 20, 19, 8, 13, 7, 1, 6, 22, 23, 11, 20, 16, 18, 17, 14, 10, 23, 9, 25,
+    1, 11, 23, 17, 15, 12, 4, 19, 3, 18, 19, 14, 21, 11, 22, 9, 25, 5, 16, 18, 20, 23, 8, 11, 20, 19, 15, 17,
+    17, 18, 14, 17, 19, 23, 21, 12, 14, 21, 6, 18, 9, 12, 15, 17, 14, 18, 3, 0, 25, 10, 19, 21, 15, 13, 20, 23,
+    22, 9, 2, 18, 13, 22, 14, 15, 22, 13, 17, 1, 19, 21, 18, 12, 20, 11, 18, 25, 8, 18, 23, 22, 14, 15, 21, 11,
 )
 
 
@@ -353,8 +353,8 @@
     y_out, dx_out, res, vec_out, tiles_hbm = refs[19:24]
     (
         at, g, give, pair, line_xy, line_z, ring, big, left, act, hid, qkv, probs, attended, branch, middle, dmid,
-        late_in, vec_w, vec_h, rstd4, sums4, vec_in, vec_own, vec_got,
-        send, recv, v_send, v_recv, p_send, p_recv, l_sem, w_in, w_keep, w_send, w_recv, t_sem, s_sem, e_sem,
+        late_in, near_left, near_right, vec_w, vec_h, rstd4, sums4, vec_in, vec_own, vec_got,
+        send, recv, v_send, v_recv, p_send, p_recv, l_sem, w_in, w_keep, w_send, w_recv, t_sem, s_sem, e_sem, n_send, n_recv,
     ) = refs[24:]
     r = lax.axis_index("rep")
     c = lax.axis_index("shard")
@@ -365,6 +365,7 @@
         "Y": {"rep": r + 2 - 4 * y},
         "U": {"rep": r + 4},
         "D": {"rep": r - 4},
+        "XY": {"rep": r + 3 - 2 * x - 4 * y},
     }
     line_end = (z == 0) | (z == 3)
     line_mid = (z == 1) | (z == 2)
@@ -387,7 +388,7 @@
                 tile_of.append((m, row, col))
     first_tile = [min(t for t, v in enumerate(tile_of) if v[0] == m) for m in range(4)]
     parts = 2 * len(tile_of)
-    slots_f, slots_b, late, slots_l, slots_g = 6, 16, 16, 3, 7
+    slots_f, slots_b, late, slots_l, slots_g = 6, 16, 16, 2, 7
 
     def part_read(i):
         m, row, col = tile_of[i // 2]
@@ -427,7 +428,7 @@
         part_read(i).start()
 
     barrier = pltpu.get_barrier_semaphore()
-    for peer in (core, to["X"], to["Y"]):
+    for peer in (core, to["X"], to["Y"], to["XY"]):
         pl.semaphore_signal(barrier, inc=1, device_id=peer, device_id_type=MESH)
 
     @pl.when(z < 3)
@@ -543,7 +544,7 @@
             lax.fori_loop(0, 8, convert, 0)
             part_keep(i).start()
             if i == 0:
-                pl.semaphore_wait(barrier, 5)
+                pl.semaphore_wait(barrier, 6)
                 small_copy(0, True).start()
                 small_copy(1, True).start()
             part_give(i).start()
@@ -556,9 +557,21 @@
                     part_read(late + k).start()
         converted[0] = max(converted[0], upto)
 
+    def cotangent_copy(k, relay):
+        here, there = pl.ds(0, length), pl.ds(length, length)
+        cols = pl.ds(g_base[3], width)
+        return pltpu.make_async_remote_copy(
+            src_ref=near_right.at[k, here, :] if relay else near_right.at[0, here, :] if k == 2 else g.at[here, cols],
+            dst_ref=near_right.at[k, there if relay else here, :],
+            send_sem=n_send.at[k, int(relay)], recv_sem=n_recv.at[k, int(relay)],
+            device_id=core if relay else to["XYY"[k]], device_id_type=MESH,
+        )
+
     convert_parts(2)
     e_copy.wait()
     right_far(3).start()
+    cotangent_copy(0, False).start()
+    cotangent_copy(1, False).start()
     convert_parts(4)
 
     def tile(m, half, index):
@@ -677,6 +690,10 @@
     turn(act, 0)
     start_left(0)
     convert_parts(16)
+    for k in range(2):
+        cotangent_copy(k, False).wait()
+        cotangent_copy(k, True).start()
+    cotangent_copy(2, False).start()
 
     low_lane = lax.broadcasted_iota(jnp.int32, (length, 128), 1) < 64
     allowed = lax.broadcasted_iota(jnp.int32, (length, length), 1) <= lax.broadcasted_iota(
@@ -770,6 +787,8 @@
             ).astype(BF16)
         return 0
 
+    cotangent_copy(2, False).wait()
+    cotangent_copy(2, True).start()
     each(hidden_norm, 16)
     for j in range(blocks):
         turn(hid.at[pl.ds(j * length, length), :], 3, j)
@@ -1021,7 +1040,7 @@
             start = pl.multiple_of(start, 16)
         return res.at[unit, pl.ds(start, count), :]
 
-    def product(unit, start, count, dest, dest_start, got=None, got_start=0):
+    def product(unit, start, count, dest, dest_start, got=None, got_start=0, near_start=None):
         m, row, col = units[unit]
         step = 128 if count % 128 == 0 else min(count, 64)
 
@@ -1033,6 +1052,14 @@
                 g[:, pl.ds(pl.multiple_of(g_base[m] + col + strip * 256, 256), 256)],
                 preferred_element_type=F32,
             )
+            if near_start is not None:
+                for peer in range(3):
+                    rows = peer * (UNIT_ROWS // 4) + near_start + part * step
+                    value = value + jnp.dot(
+                        near_left[unit, pl.ds(pl.multiple_of(rows, 16), step), :],
+                        near_right[peer, :, pl.ds(pl.multiple_of(col + strip * 256, 256), 256)],
+                        preferred_element_type=F32,
+                    )
             if got is not None:
                 value = value + got[pl.ds(pl.multiple_of(got_start + part * step, 16), step), cols].astype(F32)
             dest[pl.ds(pl.multiple_of(dest_start + part * step, 16), step), cols] = value.astype(BF16)
@@ -1086,14 +1113,24 @@
 
     def task_xy(unit, step):
         half, quarter, size = UNIT_ROWS // 2, UNIT_ROWS // 4, UNIT_ROWS // 16
-        first, second = ("X", "Y") if kinds[unit] == "X" else ("Y", "X")
-        p, q = (x, y) if kinds[unit] == "X" else (y, x)
+        first, second = ("X", "Y") if kinds[unit][-1] == "X" else ("Y", "X")
+        p, q = (x, y) if first == "X" else (y, x)
+        by_tokens = kinds[unit][0] == "Q"
         line, block, out, other = line_xy.at[xy_at[unit]], res.at[unit], give.at[pl.ds(unit * GIVE_ROWS, GIVE_ROWS), :], pair.at[unit]
         keep, away_half = p * half, (1 - p) * half
         base = keep + q * quarter
         away = keep + (1 - q) * quarter
         at_z = half + quarter
         d1 = copy(unit, "d1", out.at[pl.ds(0, half), :], rows_of(unit, away_half, half), to[first])
+
+        def left_for(peer):
+            m, row, _ = units[unit]
+            px, py = ((1 - x, y), (x, 1 - y), (1 - x, 1 - y))[peer]
+            at_p, at_q = (px, py) if first == "X" else (py, px)
+            rows = pl.ds(pl.multiple_of(at_base[m] + row + at_p * half + at_q * quarter, quarter), quarter)
+            dest = near_left.at[unit, pl.ds(peer * quarter, quarter), :]
+            return copy(unit, "d1", at.at[rows, :], dest, to[("X", "Y", "XY")[peer]])
+
         d2 = copy(unit, "d2", out.at[pl.ds(half, quarter), :], other.at[pl.ds(0, quarter), :], to[second])
         z1 = copy(unit, "z1", out.at[pl.ds(at_z, 3 * size), :], line.at[pl.ds(0, 3 * size), :], inward)
         z2 = copy(unit, "z2", out.at[pl.ds(at_z, 2 * size), :], line.at[pl.ds(3 * size, 2 * size), :], across)
@@ -1103,7 +1140,25 @@
         own_half = rows_of(unit, keep, half)
         g1 = copy(unit, "g1", own_half, own_half, to[first])
         own = base + z * size
-        if step == 0:
+        if step == 0 and by_tokens:
+            for peer in range(3):
+                left_for(peer)().start()
+        elif step == 1 and by_tokens:
+            pass
+        elif step == 2 and by_tokens:
+            arrived = near_left.at[unit]
+            copy(unit, "d1", arrived, arrived, to["X"])().wait_recv()
+
+            product(unit, base, quarter, block, base, near_start=0)
+
+            @pl.when(line_end)
+            def _():
+                from_row = pl.multiple_of(base + (1 - upper) * size, 16)
+                for n in range(3):
+                    out[at_z + n * size : at_z + (n + 1) * size, :] = block[pl.ds(from_row + n * size, size), :]
+                z1().start()
+
+        elif step == 0:
             product(unit, away_half, half, out, 0)
             d1().start()
         elif step == 1:
@@ -1163,7 +1218,8 @@
             g1().start()
         else:
             g1().wait_recv()
-            finish(unit, 2 * half + 2 * quarter + 4 * size, 2 * half + 2 * quarter + 8 * size)
+            sent = half + quarter + (3 * size if by_tokens else half + quarter)
+            finish(unit, sent + 4 * size, sent + 8 * size)
 
     def task_z(unit, step):
         size, half, quarter = UNIT_ROWS // 4, UNIT_ROWS // 8, UNIT_ROWS // 16
@@ -1250,6 +1306,9 @@
             tasks[a][1]()
         elif kind == "wait":
             wait_pair(a)
+            if a == 3:
+                for k in range(3):
+                    cotangent_copy(k, True).wait()
             if a == 1:
                 for k in range(parts):
                     given(k)
@@ -1309,7 +1368,9 @@
             pltpu.VMEM((length, width), F32),
             pltpu.VMEM((length, width), F32),
             pltpu.VMEM((length, width), F32),
-            pltpu.VMEM((3 * 256, UNIT_COLS), F32),
+            pltpu.VMEM((2 * 256, UNIT_COLS), F32),
+            pltpu.VMEM((dims[3][0] // UNIT_ROWS, 3 * UNIT_ROWS // 4, 2 * length), BF16),
+            pltpu.VMEM((3, 2 * length, width), BF16),
             pltpu.VMEM((16, width), F32),
             pltpu.VMEM((8, hidden), F32),
             pltpu.VMEM((length, 128), F32),
@@ -1331,9 +1392,11 @@
             dma((4,)),
             dma((2, 2)),
             dma((1,)),
+            dma((3, 2)),
+            dma((3, 2)),
         ],
         compiler_params=pltpu.CompilerParams(
-            collective_id=0, has_side_effects=True, vmem_limit_bytes=50 * MIB
+            collective_id=0, has_side_effects=True, vmem_limit_bytes=50 * MIB + 786432
         ),
         name="whole_layer",
     )(layer_input, cotangent, *weights, *params)

time: 222 us -> 211 us (0.950)
  Pallas kernels: 221 us -> 210 us
    pallas_call x1, Pallas kernels: 212 us -> 201 us  [whole_layer(): pl.pallas_call(functools.partial(layer_kernel, dims, at_base, g_base), ou...]
where the time goes in v5:
time: 211 us
  Pallas kernels  210 us (100%)
    pallas_call x1, Pallas kernels, whole_layer(): pl.pallas_call(functools.partial(layer_kernel, dims, at_base, g_base), ou...  201 us
    pallas_call x1, Pallas kernels, write_results(): pl.pallas_call(functools.partial(finish_kernel, dims), out_shape=[jax.Sha...  8.87 us

profile of v5, /device:TPU:0, one launch (start us, length us, event | category | flops | bytes accessed | tf_op | source)
XLA Modules:
  0.0 211.0 jit_solution(14981721166188178897)
XLA Ops:
  0.7 201.3 %whole_layer.1 = (bf16[128,1024]{1,0:T(8,128)(2,1)S(1)}, f32[128,1024]{1,0:T(8,128)S(1)}, bf16[24,256,1024]{2,1,0:T(8,128)(2,1)S(1)}, f32[24,512]{1,0:T(8,128)S(1)}, bf16[2,12,512,1024]{3,2,1,0:T(8,128)(2,1)}) custom-call(bf16[128,1024]{1,0:T(8,128)(2,1)} %refs_0_.1, bf16[128,1024]{1,0:T(8,128)(2,1)} %refs_1_.1, f32[512,3072]{1,0:T(8,128)} %refs_2_.1, ...), custom_call_target="tpu_custom_call" | custom-call | tf_op jit(solution)/shard_map/whole_layer/pallas_call | solution.py:1342
  202.0 8.9 %write_results.1 = (bf16[128,1024]{1,0:T(8,128)(2,1)}, f32[128,1024]{1,0:T(8,128)}, f32[512,3072]{1,0:T(8,128)}, f32[512,1024]{1,0:T(8,128)}, f32[512,4096]{1,0:...) custom-call(bf16[128,1024]{1,0:T(8,128)(2,1)S(1)} %get-tuple-element, ...), custom_call_target="tpu_custom_call" | custom-call | tf_op jit(solution)/shard_map/write_results/pallas_call | solution.py:1462

commit v6 on v5

--- a/solution.py
+++ b/solution.py
@@ -354,7 +354,7 @@
     (
         at, g, give, pair, line_xy, line_z, ring, big, left, act, hid, qkv, probs, attended, branch, middle, dmid,
         late_in, near_left, near_right, vec_w, vec_h, rstd4, sums4, vec_in, vec_own, vec_got,
-        send, recv, v_send, v_recv, p_send, p_recv, l_sem, w_in, w_keep, w_send, w_recv, t_sem, s_sem, e_sem, n_send, n_recv,
+        send, recv, v_send, v_recv, p_send, p_recv, l_sem, w_in, w_keep, w_send, w_recv, w_store, t_sem, s_sem, e_sem, n_send, n_recv,
     ) = refs[24:]
     r = lax.axis_index("rep")
     c = lax.axis_index("shard")
@@ -412,15 +412,25 @@
     def part_keep(i):
         return pltpu.make_async_copy(part_low(i), part_place(i), w_keep.at[i % slots_b])
 
+    def part_landing(i):
+        if i < 8:
+            return res.at[i]
+        return ring.at[(i - 8) // 2, pl.ds((i % 2) * 256, 256), :]
+
+    def part_store(i):
+        far = tiles_hbm.at[1 - c, i // 2, pl.ds((i % 2) * 256, 256), :]
+        return pltpu.make_async_copy(part_landing(i), far, w_store.at[i])
+
     def part_give(i):
         return pltpu.make_async_remote_copy(
-            src_ref=part_low(i), dst_ref=part_place(i), send_sem=w_send.at[i % slots_b], recv_sem=w_recv.at[i],
+            src_ref=part_low(i), dst_ref=part_landing(i) if i < late else part_place(i), send_sem=w_send.at[i % slots_b], recv_sem=w_recv.at[i],
             device_id=core, device_id_type=MESH,
         )
 
     def part_got(i):
         return pltpu.make_async_remote_copy(
-            src_ref=part_low(i), dst_ref=tiles_hbm.at[1 - c, i // 2, pl.ds((i % 2) * 256, 256), :],
+            src_ref=part_low(i),
+            dst_ref=part_landing(i) if i < late else tiles_hbm.at[1 - c, i // 2, pl.ds((i % 2) * 256, 256), :],
             send_sem=w_send.at[i % slots_b], recv_sem=w_recv.at[i], device_id=core, device_id_type=MESH,
         )
 
@@ -578,9 +588,6 @@
         return (half, first_tile[m] + index)
 
     stream = []
-    for m in (0, 1, 2):
-        for index in range(dims[m][1] // UNIT_COLS):
-            stream += [tile(m, 0, index), tile(m, 1, index)]
     per_half = dims[3][0] // TILE
     stream += [tile(3, h, k) for h in range(2) for k in range(per_half)]
     for m in (2, 1, 0):
@@ -602,7 +609,8 @@
             convert_parts(2 * t + 2)
             for k in (2 * t, 2 * t + 1):
                 kept(k)
-                part_got(k).wait_recv()
+                if k >= late:
+                    part_got(k).wait_recv()
         tile_load(i).start()
 
     at_tile, started, allowed_to = [0], [0], [0]
@@ -655,14 +663,20 @@
     def tn(a, b):
         return lax.dot_general(a, b, TN, preferred_element_type=F32)
 
-    def product_pair(source, write):
-        first, second = next_tile(), next_tile(1)
+    def product_pair(source, write, t):
+        convert_parts(2 * t + 2)
+        for i in (2 * t, 2 * t + 1):
+            part_got(i).wait_recv()
+            part_store(i).start()
+        far = (part_landing(2 * t), part_landing(2 * t + 1))
         for k in range(UNIT_COLS // 256):
             cols = slice(k * 256, (k + 1) * 256)
-            value = jnp.dot(source[:, 0:half_w], first[:, cols], preferred_element_type=F32)
-            value = value + jnp.dot(source[:, half_w:width], second[:, cols], preferred_element_type=F32)
+            own = low_buf[512 * t : 512 * (t + 1), cols]
+            value = jnp.dot(source[:, lane_w], own, preferred_element_type=F32)
+            for n in range(2):
+                lanes = pl.ds(pl.multiple_of((1 - c) * half_w + n * 256, 256), 256)
+                value = value + jnp.dot(source[:, lanes], far[n][:, cols], preferred_element_type=F32)
             write(cols, value)
-        done_tile(2)
 
     small_copy(0, True).wait_send()
     small_copy(1, True).wait_send()
@@ -675,7 +689,6 @@
         return 0
 
     each(first_norm, unroll=2)
-    fill(8)
     for index in range(3):
 
         def put_qkv(cols, value, index=index):
@@ -685,7 +698,7 @@
                 value = value + vec_w[VB : VB + 1, cols]
             qkv[:, index * width + cols.start : index * width + cols.stop] = value.astype(BF16)
 
-        product_pair(act, put_qkv)
+        product_pair(act, put_qkv, first_tile[0] + index)
         convert_parts(10 + 2 * index)
     turn(act, 0)
     start_left(0)
@@ -729,13 +742,11 @@
         return 0
 
     lax.fori_loop(0, width // 128 // PAIRS, attend_some, 0)
-    fill(10)
 
     def put_branch(cols, value):
         branch[:, cols] = value + vec_w[OB : OB + 1, cols]
 
-    product_pair(act, put_branch)
-    fill(16)
+    product_pair(act, put_branch, first_tile[1])
     turn(act, 1)
     start_left(1)
 
@@ -755,7 +766,7 @@
             wide = slice(j * width + cols.start, j * width + cols.stop)
             big[U0 + j * length : U0 + (j + 1) * length, cols] = value + vec_h[UB : UB + 1, wide]
 
-        product_pair(act, put_hidden)
+        product_pair(act, put_hidden, first_tile[2] + j)
     turn(act, 2)
     start_left(2)
     root_half = 0.7071067811865476
@@ -794,6 +805,8 @@
         turn(hid.at[pl.ds(j * length, length), :], 3, j)
     start_left(3)
     convert_parts(parts)
+    for i in range(late):
+        part_store(i).wait()
 
     tasks = []
     zeros8 = jnp.zeros((8, width), F32)
@@ -1389,6 +1402,7 @@
             dma((16,)),
             dma((16,)),
             dma((2 * tiles,)),
+            dma((16,)),
             dma((4,)),
             dma((2, 2)),
             dma((1,)),

time: 211 us -> 206 us (0.976)
  Pallas kernels: 210 us -> 205 us
    pallas_call x1, Pallas kernels: 201 us -> 196 us  [whole_layer(): pl.pallas_call(functools.partial(layer_kernel, dims, at_base, g_base), ou...]
where the time goes in v6:
time: 206 us
  Pallas kernels  205 us (100%)
    pallas_call x1, Pallas kernels, whole_layer(): pl.pallas_call(functools.partial(layer_kernel, dims, at_base, g_base), ou...  196 us
    pallas_call x1, Pallas kernels, write_results(): pl.pallas_call(functools.partial(finish_kernel, dims), out_shape=[jax.Sha...  8.87 us

profile of v6, /device:TPU:0, one launch (start us, length us, event | category | flops | bytes accessed | tf_op | source)
XLA Modules:
  0.0 206.2 jit_solution(9419267911579250192)
XLA Ops:
  0.7 196.5 %whole_layer.1 = (bf16[128,1024]{1,0:T(8,128)(2,1)S(1)}, f32[128,1024]{1,0:T(8,128)S(1)}, bf16[24,256,1024]{2,1,0:T(8,128)(2,1)S(1)}, f32[24,512]{1,0:T(8,128)S(1)}, bf16[2,12,512,1024]{3,2,1,0:T(8,128)(2,1)}) custom-call(bf16[128,1024]{1,0:T(8,128)(2,1)} %refs_0_.1, bf16[128,1024]{1,0:T(8,128)(2,1)} %refs_1_.1, f32[512,3072]{1,0:T(8,128)} %refs_2_.1, ...), custom_call_target="tpu_custom_call" | custom-call | tf_op jit(solution)/shard_map/whole_layer/pallas_call | solution.py:1355
  197.2 8.9 %write_results.1 = (bf16[128,1024]{1,0:T(8,128)(2,1)}, f32[128,1024]{1,0:T(8,128)}, f32[512,3072]{1,0:T(8,128)}, f32[512,1024]{1,0:T(8,128)}, f32[512,4096]{1,0:...) custom-call(bf16[128,1024]{1,0:T(8,128)(2,1)S(1)} %get-tuple-element, ...), custom_call_target="tpu_custom_call" | custom-call | tf_op jit(solution)/shard_map/write_results/pallas_call | solution.py:1476

commit v7 on v6

--- a/solution.py
+++ b/solution.py
@@ -388,7 +388,7 @@
                 tile_of.append((m, row, col))
     first_tile = [min(t for t, v in enumerate(tile_of) if v[0] == m) for m in range(4)]
     parts = 2 * len(tile_of)
-    slots_f, slots_b, late, slots_l, slots_g = 6, 16, 16, 2, 7
+    slots_f, slots_b, late, slots_l, slots_g = 6, 16, 16, 2, 6
 
     def part_read(i):
         m, row, col = tile_of[i // 2]
@@ -399,7 +399,7 @@
         )
 
     def low_row(i):
-        return 240 * 16 + (i - late) % slots_g * 256 if i >= late else i * 256
+        return (late + (i - late) % slots_g) * 256 if i >= late else i * 256
 
     def part_low(i):
         return low_buf.at[pl.ds(low_row(i), 256), :]
@@ -536,10 +536,7 @@
             part_read(i).wait()
             if i >= slots_b:
                 kept(i - slots_b)
-            if i == late:
-                for k in range(late):
-                    kept(k)
-                    given(k)
+                given(i - slots_b)
             if i >= late + slots_g:
                 kept(i - slots_g)
                 given(i - slots_g)
@@ -767,6 +764,7 @@
             big[U0 + j * length : U0 + (j + 1) * length, cols] = value + vec_h[UB : UB + 1, wide]
 
         product_pair(act, put_hidden, first_tile[2] + j)
+        convert_parts(min(late + 2 * (j + 1), late + slots_g))
     turn(act, 2)
     start_left(2)
     root_half = 0.7071067811865476
@@ -807,6 +805,8 @@
     convert_parts(parts)
     for i in range(late):
         part_store(i).wait()
+        kept(i)
+        given(i)
 
     tasks = []
     zeros8 = jnp.zeros((8, width), F32)

time: 206 us -> 205 us (level)
  no operation moved by 1% of the time
where the time goes in v7:
time: 205 us
  Pallas kernels  204 us (100%)
    pallas_call x1, Pallas kernels, whole_layer(): pl.pallas_call(functools.partial(layer_kernel, dims, at_base, g_base), ou...  195 us
    pallas_call x1, Pallas kernels, write_results(): pl.pallas_call(functools.partial(finish_kernel, dims), out_shape=[jax.Sha...  8.87 us

profile of v7, /device:TPU:0, one launch (start us, length us, event | category | flops | bytes accessed | tf_op | source)
XLA Modules:
  0.0 205.0 jit_solution(14829697066646075659)
XLA Ops:
  0.7 195.3 %whole_layer.1 = (bf16[128,1024]{1,0:T(8,128)(2,1)S(1)}, f32[128,1024]{1,0:T(8,128)S(1)}, bf16[24,256,1024]{2,1,0:T(8,128)(2,1)S(1)}, f32[24,512]{1,0:T(8,128)S(1)}, bf16[2,12,512,1024]{3,2,1,0:T(8,128)(2,1)}) custom-call(bf16[128,1024]{1,0:T(8,128)(2,1)} %refs_0_.1, bf16[128,1024]{1,0:T(8,128)(2,1)} %refs_1_.1, f32[512,3072]{1,0:T(8,128)} %refs_2_.1, ...), custom_call_target="tpu_custom_call" | custom-call | tf_op jit(solution)/shard_map/whole_layer/pallas_call | solution.py:1355
  196.0 8.9 %write_results.1 = (bf16[128,1024]{1,0:T(8,128)(2,1)}, f32[128,1024]{1,0:T(8,128)}, f32[512,3072]{1,0:T(8,128)}, f32[512,1024]{1,0:T(8,128)}, f32[512,4096]{1,0:...) custom-call(bf16[128,1024]{1,0:T(8,128)(2,1)S(1)} %get-tuple-element, ...), custom_call_target="tpu_custom_call" | custom-call | tf_op jit(solution)/shard_map/write_results/pallas_call | solution.py:1476

commit v8 on v7

--- a/solution.py
+++ b/solution.py
@@ -338,7 +338,7 @@
     return order
 
 
-PAIRS = 2
+PAIRS = 4
 
 
 def fold(v):

time: 205 us -> 204 us (level)
  no operation moved by 1% of the time
where the time goes in v8:
time: 204 us
  Pallas kernels  203 us (100%)
    pallas_call x1, Pallas kernels, whole_layer(): pl.pallas_call(functools.partial(layer_kernel, dims, at_base, g_base), ou...  194 us
    pallas_call x1, Pallas kernels, write_results(): pl.pallas_call(functools.partial(finish_kernel, dims), out_shape=[jax.Sha...  8.87 us

profile of v8, /device:TPU:0, one launch (start us, length us, event | category | flops | bytes accessed | tf_op | source)
XLA Modules:
  0.0 203.5 jit_solution(2346644484183791771)
XLA Ops:
  0.7 193.8 %whole_layer.1 = (bf16[128,1024]{1,0:T(8,128)(2,1)S(1)}, f32[128,1024]{1,0:T(8,128)S(1)}, bf16[24,256,1024]{2,1,0:T(8,128)(2,1)S(1)}, f32[24,512]{1,0:T(8,128)S(1)}, bf16[2,12,512,1024]{3,2,1,0:T(8,128)(2,1)}) custom-call(bf16[128,1024]{1,0:T(8,128)(2,1)} %refs_0_.1, bf16[128,1024]{1,0:T(8,128)(2,1)} %refs_1_.1, f32[512,3072]{1,0:T(8,128)} %refs_2_.1, ...), custom_call_target="tpu_custom_call" | custom-call | tf_op jit(solution)/shard_map/whole_layer/pallas_call | solution.py:1355
  194.5 8.9 %write_results.1 = (bf16[128,1024]{1,0:T(8,128)(2,1)}, f32[128,1024]{1,0:T(8,128)}, f32[512,3072]{1,0:T(8,128)}, f32[512,1024]{1,0:T(8,128)}, f32[512,4096]{1,0:...) custom-call(bf16[128,1024]{1,0:T(8,128)(2,1)S(1)} %get-tuple-element, ...), custom_call_target="tpu_custom_call" | custom-call | tf_op jit(solution)/shard_map/write_results/pallas_call | solution.py:1476
